TPU v7x, 256 devices: a whole 4x4x8 slice. The times are simulated.
256 devices in a mesh: dp: 32 (over z_hi, x, core), tensor: 8 (over z_lo, y).
Axes of the slice: x: 4, y: 4, z: 8 (z_hi: 4, z_lo: 2; z = z_hi * 2 + z_lo), core: 2. Of those that a mesh axis runs over, the one named last changes fastest.
Arguments:
- tokens: bfloat16 [32768, 2048], P('dp', 'tensor'), may hold values from -6 to 6
- gain: bfloat16 [2048], replicated, may hold values from 0.099609375 to 1.8984375
- gate_weight: bfloat16 [2048, 7168], P(None, 'tensor'), may hold values from -0.125 to 0.125
- up_weight: bfloat16 [2048, 7168], P(None, 'tensor'), may hold values from -0.125 to 0.125
- down_weight: bfloat16 [7168, 2048], P('tensor'), may hold values from -0.0625 to 0.0625
- cotangent: bfloat16 [32768, 2048], P('dp', 'tensor'), may hold values from -6 to 6
- lengths: int32 [64], P('dp'), may hold values from 1 to 512, 8192 in all
Outputs:
- layer_out: bfloat16 [32768, 2048], P('dp', 'tensor')
- input_grad: bfloat16 [32768, 2048], P('dp', 'tensor')
Inputs may be any that keep to these rules, and one draw needn't show every extreme that they name: The lengths sum to exactly 8192; at least one sequence has exactly 512 tokens.
All inputs are finite; a program needn't handle non-finite values. No bound on the sum of `lengths` on one device may be relied on, other than what follows from the above.
Results may differ from a plain program's by a relative error of at most 0.015.
Values may be sent and summed in bfloat16 or wider, within the bound.
A program may use at most 128 MiB of HBM per device.

v0:
```python
import jax
import jax.numpy as jnp
from jax import lax
from jax.sharding import PartitionSpec as P

TOK_DEV = 256


EPSILON = 1e-05


def lookup_small(index_values, table):
    picks = index_values[..., None] == jnp.arange(table.shape[0], dtype=jnp.int32)
    return jnp.sum(jnp.where(picks, table, 0), axis=-1)


def count_below(values, bounds):
    return jnp.sum((values[..., None] >= bounds).astype(jnp.int32), axis=-1)


def layer_core(token_part, cotan_part, gain, gate_weight, up_weight, down_weight):
    width_part = token_part.shape[1]
    lane_index = lax.axis_index("tensor")
    token_full, cotan_full = (
        lax.all_gather(token_part, "tensor", axis=1, tiled=True),
        lax.all_gather(cotan_part, "tensor", axis=1, tiled=True),
    )
    xfloat = token_full.astype(jnp.float32)
    scaler = lax.rsqrt(jnp.mean(xfloat * xfloat, axis=1, keepdims=True) + EPSILON)
    unit_rows = xfloat * scaler
    gain_float = gain.astype(jnp.float32)
    normed = (unit_rows * gain_float).astype(jnp.bfloat16)
    gate_values = jnp.dot(normed, gate_weight, preferred_element_type=jnp.float32)
    up_values = jnp.dot(normed, up_weight, preferred_element_type=jnp.float32)
    sigmoid = jax.nn.sigmoid(gate_values)
    activation = gate_values * sigmoid
    hidden = (activation * up_values).astype(jnp.bfloat16)
    layer_terms = jnp.dot(hidden, down_weight, preferred_element_type=jnp.float32)
    layer_sum = lax.psum_scatter(
        layer_terms.astype(jnp.bfloat16), "tensor", scatter_dimension=1, tiled=True
    ).astype(jnp.float32)
    layer_part = (token_part.astype(jnp.float32) + layer_sum).astype(jnp.bfloat16)
    contract_last = (((1,), (1,)), ((), ()))
    hidden_grad = lax.dot_general(
        cotan_full, down_weight, contract_last, preferred_element_type=jnp.float32
    )
    gate_grad = (hidden_grad * up_values * sigmoid * (1.0 + gate_values * (1.0 - sigmoid))).astype(
        jnp.bfloat16
    )
    up_grad = (hidden_grad * activation).astype(jnp.bfloat16)
    normed_terms = lax.dot_general(
        gate_grad, gate_weight, contract_last, preferred_element_type=jnp.float32
    )
    normed_terms = normed_terms + lax.dot_general(
        up_grad, up_weight, contract_last, preferred_element_type=jnp.float32
    )
    column_start = lane_index * width_part
    normed_grad = lax.psum(normed_terms, "tensor")
    unit_grad = normed_grad * gain_float
    inner_mean = jnp.mean(unit_grad * unit_rows, axis=1, keepdims=True)
    full_grad = scaler * (unit_grad - unit_rows * inner_mean)
    part_grad = lax.dynamic_slice_in_dim(full_grad, column_start, width_part, 1)
    grad_part = (cotan_part.astype(jnp.float32) + part_grad).astype(jnp.bfloat16)
    return (layer_part, grad_part)


def shards(tokens, gain, gate_weight, up_weight, down_weight, cotangent, lengths):
    row_total, width_part = tokens.shape
    seq_count = lengths.shape[0]
    seq_length = row_total // seq_count
    row_ids = jnp.arange(row_total, dtype=jnp.int32)
    row_seq = row_ids // seq_length
    row_pos = row_ids % seq_length
    row_limit = lookup_small(row_seq, lengths)
    is_valid = row_pos < row_limit
    members = lax.axis_size("dp")
    my_index = lax.axis_index("dp")
    own_count = jnp.sum(lengths)
    all_counts = lax.all_gather(own_count.reshape(1), "dp", axis=0, tiled=True)
    count_ends = jnp.cumsum(all_counts)
    count_starts = count_ends - all_counts
    own_start = lookup_small(my_index, count_starts)
    slot_count = (row_total + members - 2) // members + 1
    seq_ends = jnp.cumsum(lengths)
    seq_starts = seq_ends - lengths
    peer_ids = jnp.arange(members, dtype=jnp.int32)[:, None]
    slot_ids = jnp.arange(slot_count, dtype=jnp.int32)[None, :]
    global_rank = (own_start // members + slot_ids) * members + peer_ids
    local_rank = global_rank - own_start
    is_sent = (local_rank >= 0) & (local_rank < own_count)
    local_safe = jnp.where(is_sent, local_rank, 0)
    send_seq = count_below(local_safe, seq_ends)
    send_row = send_seq * seq_length + local_safe - lookup_small(send_seq, seq_starts)
    flat_rows = send_row.reshape(-1)

    def pack_rows(source):
        picked = jnp.take(source, flat_rows, axis=0).reshape(members, slot_count, width_part)
        return jnp.where(is_sent[:, :, None], picked, jnp.zeros_like(picked))

    got_tokens, got_cotan = (
        lax.all_to_all(pack_rows(tokens), "dp", split_axis=0, concat_axis=0, tiled=True),
        lax.all_to_all(pack_rows(cotangent), "dp", split_axis=0, concat_axis=0, tiled=True),
    )
    packed_ids = jnp.arange(TOK_DEV, dtype=jnp.int32)
    packed_rank = packed_ids * members + my_index
    source_ids = count_below(packed_rank, count_ends)
    source_start = lookup_small(source_ids, count_starts)
    recv_flat = source_ids * slot_count + packed_ids - source_start // members
    token_packed = jnp.take(got_tokens.reshape(members * slot_count, width_part), recv_flat, axis=0)
    cotan_packed = jnp.take(got_cotan.reshape(members * slot_count, width_part), recv_flat, axis=0)
    layer_packed, grad_packed = layer_core(
        token_packed, cotan_packed, gain, gate_weight, up_weight, down_weight
    )

    def unpack_slots(values):
        empty = jnp.zeros((members * slot_count, width_part), values.dtype)
        return empty.at[recv_flat].set(values).reshape(members, slot_count, width_part)

    back_layer, back_grad = (
        lax.all_to_all(unpack_slots(layer_packed), "dp", split_axis=0, concat_axis=0, tiled=True),
        lax.all_to_all(unpack_slots(grad_packed), "dp", split_axis=0, concat_axis=0, tiled=True),
    )
    row_rank = own_start + lookup_small(row_seq, seq_starts) + row_pos
    back_flat = row_rank % members * slot_count + row_rank // members - own_start // members
    back_flat = jnp.where(is_valid, back_flat, 0)
    layer_rows = jnp.take(back_layer.reshape(members * slot_count, width_part), back_flat, axis=0)
    grad_rows = jnp.take(back_grad.reshape(members * slot_count, width_part), back_flat, axis=0)
    zero_rows = jnp.zeros_like(tokens)
    layer_out = jnp.where(is_valid[:, None], layer_rows, zero_rows)
    input_grad = jnp.where(is_valid[:, None], grad_rows, zero_rows)
    return (layer_out, input_grad)


def solution(mesh):
    placed = (
        P("dp", "tensor"),
        P(),
        P(None, "tensor"),
        P(None, "tensor"),
        P("tensor", None),
        P("dp", "tensor"),
        P("dp"),
    )
    return jax.shard_map(
        shards,
        mesh=mesh,
        in_specs=placed,
        out_specs=(P("dp", "tensor"), P("dp", "tensor")),
        check_vma=False,
    )
```

profile of v0, /device:TPU:1, one launch (start us, length us, event | category | flops | bytes accessed | tf_op | source)
XLA Modules:
  0.0 373.4 jit_solution(4411851426015422699)
XLA Ops:
  7.2 0.9 reduce-window.17
  8.1 1.3 bitcast_subtract_fusion
  9.4 1.3 dynamic-slice
  10.6 1.4 dynamic-update-slice
  12.0 18.6 %all-reduce = s32[32]{0:T(128)S(1)} all-reduce(s32[32]{0:T(128)S(1)} %dynamic-update-slice), channel_id=1, replica_groups=mesh['dp'=32,'tensor'=8] {'dp'}, use_global_device_ids=true, to_apply=%add | all-reduce | flops 32 | bytes 256
  30.9 0.7 fusion.36
  34.1 1.3 fusion.21
  35.4 1.3 add_subtract_fusion
  37.2 0.7 compare_and_fusion
  37.9 4.1 %gather_fusion.3 = bf16[1056,256]{1,0:T(8,128)(2,1)S(1)} fusion(bf16[1024,256]{1,0:T(8,128)(2,1)S(1)} %copy-done, s32[2048]{0:T(1024)S(1)} %pad_clamp_fusion), kind=kCustom, calls=%fused_computation.3.clone | custom fusion | bytes 1085568 | tf_op jit(solution)/shard_map/jit(_take)/gather | solution.py:97
  42.0 4.1 %gather_fusion = bf16[1056,256]{1,0:T(8,128)(2,1)S(1)} fusion(bf16[1024,256]{1,0:T(8,128)(2,1)S(1)} %copy-done.1, s32[2048]{0:T(1024)S(1)} %pad_clamp_fusion), kind=kCustom, calls=%fused_computation.clone | custom fusion | bytes 1085568 | tf_op jit(solution)/shard_map/jit(_take)/gather | solution.py:97
  46.2 0.2 broadcast_select_fusion.2
  46.8 1.1 broadcast_select_fusion
  47.8 26.9 %all_to_all.20 = bf16[32,33,256]{2,1,0:T(8,128)(2,1)S(1)} all-to-all(bf16[32,33,256]{2,1,0:T(8,128)(2,1)S(1)} %get-tuple-element.19), channel_id=1, replica_groups=mesh['dp'=32,'tensor'=8] {'dp'}, dimensions={0} | all-to-all | bytes 1081344 | tf_op jit(solution)/shard_map/all_to_all | solution.py:102
  74.7 5.1 %all-to-all-start = ((bf16[32,33,256]{2,1,0:T(8,128)(2,1)}), bf16[32,33,256]{2,1,0:T(8,128)(2,1)S(1)}, u32[]{:S(2)}, u32[]{:S(2)}) async-start(bf16[32,33,256]{2,1,0:T(8,128)(2,1)} %get-tuple-element.20), calls=%async_computation | async-start | bytes 1310720 | tf_op jit(solution)/shard_map/all_to_all | solution.py:101
  80.1 0.2 reshape.283
  80.3 1.2 gather_fusion.4
  81.4 18.1 %all-to-all-done = bf16[32,33,256]{2,1,0:T(8,128)(2,1)S(1)} async-done(((bf16[32,33,256]{2,1,0:T(8,128)(2,1)}), bf16[32,33,256]{2,1,0:T(8,128)(2,1)S(1)}, u32[]{:S(2)}, u32[]{:S(2)}) %all-to-all-start) | async-done | bytes 540704 | tf_op jit(solution)/shard_map/all_to_all | solution.py:101
  99.5 0.2 reshape.279
  99.7 1.2 gather_fusion.1
  100.8 0.8 broadcast_select_fusion.4
  101.7 0.7 all-gather.5.cloned.1.call-update
  102.5 32.4 %all-gather.3.cloned.1.call-done = bf16[256,2048]{1,0:T(8,128)(2,1)} async-done(((bf16[256,256]{1,0:T(8,128)(2,1)}), bf16[256,2048]{1,0:T(8,128)(2,1)}) %all-gather.3.cloned.1.call-update) | async-done | bytes 1048592 | tf_op jit(solution)/shard_map/all_gather | solution.py:25
  134.9 1.5 fusion
  136.5 3.8 %fusion.5 = f32[256,896]{1,0:T(8,128)S(1)} fusion(bf16[2048,896]{1,0:T(8,128)(2,1)} %param.15, f32[2048]{0:T(1024)S(1)} %convert_element_type.46, bf16[256,2048]{1,0:T(8,128)(2,1)} %all-gather.3.cloned.1.call-done, f32[256]{0:T(256)S(1)} %add_rsqrt_fusion), kind=kOutput, calls=%fused_computation.30 | convolution fusion | flops 941621248 | bytes 5645312 | tf_op jit(solution)/shard_map/dot_general | solution.py:33
  140.3 1.3 fusion.4
  141.6 1.0 copy-done.11
  142.6 2.3 convolution_convert_fusion
  144.9 0.2 all-reduce.3.cloned.1.call-start
  145.2 33.0 %all-gather.5.cloned.1.call-done = bf16[256,2048]{1,0:T(8,128)(2,1)} async-done(((bf16[256,256]{1,0:T(8,128)(2,1)}), bf16[256,2048]{1,0:T(8,128)(2,1)}) %all-gather.5.cloned.1.call-update) | async-done | bytes 1048592 | tf_op jit(solution)/shard_map/all_gather | solution.py:26
  178.2 3.8 %fusion.41 = f32[256,896]{1,0:T(8,128)S(1)} fusion(bf16[256,2048]{1,0:T(8,128)(2,1)} %all-gather.5.cloned.1.call-done, bf16[896,2048]{1,0:T(8,128)(2,1)} %param.17), kind=kOutput, calls=%fused_computation.115 | convolution fusion | flops 939524096 | bytes 5636096 | tf_op jit(solution)/shard_map/dot_general | solution.py:44
  182.0 2.7 fusion.2
  184.7 2.6 convolution_add_fusion
  187.4 35.2 %reduce-scatter.2.cloned.1.call-done = bf16[256,256]{1,0:T(8,128)(2,1)} async-done(((bf16[256,2048]{1,0:T(8,128)(2,1)}), bf16[256,256]{1,0:T(8,128)(2,1)}) %reduce-scatter.2.cloned.1.call-update) | async-done | bytes 131088 | tf_op jit(solution)/shard_map/reduce_scatter | solution.py:39
  222.5 2.0 scatter_custom_fusion
  224.6 1.0 reshape.280
  225.6 14.2 %all-to-all-start.1 = ((bf16[32,33,256]{2,1,0:T(8,128)(2,1)}), bf16[32,33,256]{2,1,0:T(8,128)(2,1)S(1)}, u32[]{:S(2)}, u32[]{:S(2)}) async-start(bf16[32,33,256]{2,1,0:T(8,128)(2,1)} %reshape.280), calls=%async_computation.2 | async-start | bytes 1310720 | tf_op jit(solution)/shard_map/all_to_all | solution.py:120
  239.9 82.7 %all-reduce.3.cloned.1.call-done = f32[256,2048]{1,0:T(8,128)} async-done(((f32[256,2048]{1,0:T(8,128)}), f32[256,2048]{1,0:T(8,128)}) %all-reduce.3.cloned.1.call-update) | async-done | bytes 2097168 | tf_op jit(solution)/shard_map/psum | solution.py:58
  322.5 4.0 %multiply_reduce_fusion = (f32[256]{0:T(256)S(1)}, f32[256,2048]{1,0:T(8,128)}, f32[256,2048]{1,0:T(8,128)}) fusion(f32[256]{0:T(256)S(1)} %add_rsqrt_fusion, bf16[256,2048]{1,0:T(8,128)(2,1)S(1)} %copy-done.2, f32[256,2048]{1,0:T(8,128)} %all-reduce.3.cloned.1.call-done, f32[2048]{0:T(1024)S(1)} %convert_element_type.46), kind=kLoop, calls=%fused_computation.13 | loop fusion | flops 2621184 | bytes 7350272 | tf_op jit(solution)/shard_map/reduce_sum | solution.py:60
  326.6 2.2 scatter_custom_fusion.1
  328.8 1.0 reshape.284
  329.8 12.9 %all-to-all-start.3 = ((bf16[32,33,256]{2,1,0:T(8,128)(2,1)}), bf16[32,33,256]{2,1,0:T(8,128)(2,1)S(1)}, u32[]{:S(2)}, u32[]{:S(2)}) async-start(bf16[32,33,256]{2,1,0:T(8,128)(2,1)} %reshape.284), calls=%async_computation.4 | async-start | bytes 1310720 | tf_op jit(solution)/shard_map/all_to_all | solution.py:121
  342.9 0.6 compare_and_fusion.1
  343.6 0.2 reshape.281
  343.8 3.9 %gather_fusion.2 = bf16[1024,256]{1,0:T(8,128)(2,1)S(1)} fusion(bf16[1056,256]{1,0:T(8,128)(2,1)S(1)} %reshape.281, s32[1024]{0:T(1024)S(1)} %broadcast_clamp_fusion), kind=kCustom, calls=%fused_computation.2.clone | custom fusion | bytes 1052672 | tf_op jit(solution)/shard_map/jit(_take)/gather | solution.py:126
  347.7 13.4 %all-to-all-done.3 = bf16[32,33,256]{2,1,0:T(8,128)(2,1)S(1)} async-done(((bf16[32,33,256]{2,1,0:T(8,128)(2,1)}), bf16[32,33,256]{2,1,0:T(8,128)(2,1)S(1)}, u32[]{:S(2)}, u32[]{:S(2)}) %all-to-all-start.3) | async-done | bytes 540704 | tf_op jit(solution)/shard_map/all_to_all | solution.py:121
  361.3 3.9 %gather_fusion.5 = bf16[1024,256]{1,0:T(8,128)(2,1)S(1)} fusion(bf16[1056,256]{1,0:T(8,128)(2,1)S(1)} %reshape.285, s32[1024]{0:T(1024)S(1)} %broadcast_clamp_fusion), kind=kCustom, calls=%fused_computation.5.clone | custom fusion | bytes 1052672 | tf_op jit(solution)/shard_map/jit(_take)/gather | solution.py:127
  365.3 1.6 select_select_fusion
  (58 shorter events, 1.9 us)
Async XLA Ops:
  7.2 30.7 %copy-start = (bf16[1024,256]{1,0:T(8,128)(2,1)S(1)}, bf16[1024,256]{1,0:T(8,128)(2,1)}, u32[]{:S(2)}) copy-start(bf16[1024,256]{1,0:T(8,128)(2,1)} %param.18) | copy-start | bytes 1572868
  37.8 4.2 %copy-start.1 = (bf16[1024,256]{1,0:T(8,128)(2,1)S(1)}, bf16[1024,256]{1,0:T(8,128)(2,1)}, u32[]{:S(2)}) copy-start(bf16[1024,256]{1,0:T(8,128)(2,1)} %param.13) | copy-start | bytes 1572868
  74.7 24.8 %all-to-all-start = ((bf16[32,33,256]{2,1,0:T(8,128)(2,1)}), bf16[32,33,256]{2,1,0:T(8,128)(2,1)S(1)}, u32[]{:S(2)}, u32[]{:S(2)}) async-start(bf16[32,33,256]{2,1,0:T(8,128)(2,1)} %get-tuple-element.20), calls=%async_computation | async-start | bytes 1310720 | tf_op jit(solution)/shard_map/all_to_all | solution.py:101
  79.8 55.1 %all-gather.3.cloned.1.call-start = ((), (), s32[]{:S(2)}) async-start(), calls=%async_computation.5 | async-start | bytes 1179648 | tf_op jit(solution)/shard_map/all_gather | solution.py:25
  80.3 22.2 %copy-start.7 = (bf16[2048]{0:T(1024)(128)(2,1)S(1)}, bf16[2048]{0:T(1024)(128)(2,1)}, u32[]{:S(2)}) copy-start(bf16[2048]{0:T(1024)(128)(2,1)} %param.14) | copy-start | bytes 12292
  101.7 76.5 %all-gather.5.cloned.1.call-start = ((), (), s32[]{:S(2)}) async-start(), calls=%async_computation.7 | async-start | bytes 1179648 | tf_op jit(solution)/shard_map/all_gather | solution.py:26
  102.4 120.1 %reduce-scatter.2.cloned.1.call-start = ((), (), s32[]{:S(2)}) async-start(), calls=%async_computation.6 | async-start | bytes 1179648 | tf_op jit(solution)/shard_map/reduce_scatter | solution.py:39
  136.4 3.8 %copy-start.2 = (bf16[256,2048]{1,0:T(8,128)(2,1)S(1)}, bf16[256,2048]{1,0:T(8,128)(2,1)}, u32[]{:S(2)}) copy-start(bf16[256,2048]{1,0:T(8,128)(2,1)} %all-gather.3.cloned.1.call-done) | copy-start | bytes 3145732
  136.5 3.8 %copy-start.3 = (bf16[2048,896]{1,0:T(8,128)(2,1)S(1)}, bf16[2048,896]{1,0:T(8,128)(2,1)}, u32[]{:S(2)}) copy-start(bf16[2048,896]{1,0:T(8,128)(2,1)} %param.16) | copy-start | bytes 11010052
  140.3 2.3 copy-start.9
  141.6 1.0 copy-start.11
  144.9 177.6 %all-reduce.3.cloned.1.call-start = ((), (), s32[]{:S(2)}) async-start(), calls=%async_computation.8 | async-start | bytes 4194304 | tf_op jit(solution)/shard_map/psum | solution.py:58
  178.2 3.8 %copy-start.10 = (bf16[2048,896]{1,0:T(8,128)(2,1)S(1)}, bf16[2048,896]{1,0:T(8,128)(2,1)}, u32[]{:S(2)}) copy-start(bf16[2048,896]{1,0:T(8,128)(2,1)} %param.15) | copy-start | bytes 11010052
  182.0 2.7 copy-start.4
  187.3 35.2 %copy-start.6 = (bf16[256,256]{1,0:T(8,128)(2,1)S(1)}, bf16[256,256]{1,0:T(8,128)(2,1)}, u32[]{:S(2)}) copy-start(bf16[256,256]{1,0:T(8,128)(2,1)} %get-tuple-element.26) | copy-start | bytes 393220
  225.6 104.2 %all-to-all-start.1 = ((bf16[32,33,256]{2,1,0:T(8,128)(2,1)}), bf16[32,33,256]{2,1,0:T(8,128)(2,1)S(1)}, u32[]{:S(2)}, u32[]{:S(2)}) async-start(bf16[32,33,256]{2,1,0:T(8,128)(2,1)} %reshape.280), calls=%async_computation.2 | async-start | bytes 1310720 | tf_op jit(solution)/shard_map/all_to_all | solution.py:120
  239.8 86.7 %copy-start.5 = (bf16[256,256]{1,0:T(8,128)(2,1)S(1)}, bf16[256,256]{1,0:T(8,128)(2,1)}, u32[]{:S(2)}) copy-start(bf16[256,256]{1,0:T(8,128)(2,1)} %get-tuple-element.25) | copy-start | bytes 393220
  326.5 16.2 %copy-start.8 = (s32[2]{0:T(128)S(1)}, s32[2]{0:T(128)}, u32[]{:S(2)}) copy-start(s32[2]{0:T(128)} %param.19) | copy-start | bytes 28
  329.8 31.3 %all-to-all-start.3 = ((bf16[32,33,256]{2,1,0:T(8,128)(2,1)}), bf16[32,33,256]{2,1,0:T(8,128)(2,1)S(1)}, u32[]{:S(2)}, u32[]{:S(2)}) async-start(bf16[32,33,256]{2,1,0:T(8,128)(2,1)} %reshape.284), calls=%async_computation.4 | async-start | bytes 1310720 | tf_op jit(solution)/shard_map/all_to_all | solution.py:121
Sparse Core Ops, SparseCore 0:
  101.8 33.0 all-gather.2
  137.2 40.9 all-gather.4
  180.7 41.7 reduce-scatter.1
  225.1 97.4 all-reduce.2
where the time goes:
time: 375 us; the launch traced here: 373 us
  waiting for transfers between devices  216 us (58%)
  blocking collectives  45.5 us (12%)
  starting transfers between devices  32.6 us (9%)
  local copies, waits for them, and re-layouts  25.7 us (7%)
  other arithmetic  20.8 us (6%)
  between operations  16.7 us (4%)
  matrix products  16.5 us (4%)
    psum x1, waiting for transfers between devices, layer_core(): normed_grad = lax.psum(normed_terms, 'tensor')  82.7 us
    reduce_scatter x1, waiting for transfers between devices, layer_core(): lax.psum_scatter(layer_terms.astype(jnp.bfloat16), 'tensor', scatter_dime...  35.2 us
    all_gather x1, waiting for transfers between devices, layer_core(): lax.all_gather(cotan_part, 'tensor', axis=1, tiled=True)  33 us
    all_gather x1, waiting for transfers between devices, layer_core(): lax.all_gather(token_part, 'tensor', axis=1, tiled=True)  32.4 us
    all_to_all x1, blocking collectives, shards(): lax.all_to_all(pack_rows(cotangent), 'dp', split_axis=0, concat_axis=0, t...  26.9 us
    unnamed x1, blocking collectives  18.6 us
    all_to_all x1, waiting for transfers between devices, shards(): lax.all_to_all(pack_rows(tokens), 'dp', split_axis=0, concat_axis=0, tile...  18.1 us
    all_to_all x1, starting transfers between devices, shards(): lax.all_to_all(unpack_slots(layer_packed), 'dp', split_axis=0, concat_axi...  14.2 us
  transfers between devices with their start and end apart: 7, of which 6 were waited for; matrix products, arithmetic and copies ran while one was open for 9% of the time, Pallas kernels for 0%

commit v1 on v0

--- a/solution.py
+++ b/solution.py
@@ -1,12 +1,402 @@
+import functools
+
 import jax
 import jax.numpy as jnp
 from jax import lax
+from jax.experimental import pallas as pl
+from jax.experimental.pallas import tpu as pltpu
 from jax.sharding import PartitionSpec as P
 
 TOK_DEV = 256
-
-
 EPSILON = 1e-05
+GROUP = 8
+TILE = 8
+CAPACITIES = (320, 352, 384, 448, 512)
+MESH = pl.DeviceIdType.MESH
+NT = (((1,), (1,)), ((), ()))
+
+
+def remote(src, dst, send_sem, recv_sem, dp, tensor):
+    return pltpu.make_async_remote_copy(
+        src_ref=src, dst_ref=dst, send_sem=send_sem, recv_sem=recv_sem,
+        device_id=(dp, tensor), device_id_type=MESH,
+    )
+
+
+def signal(sem, dp, tensor):
+    pl.semaphore_signal(sem, inc=1, device_id=(dp, tensor), device_id_type=MESH)
+
+
+def exchange_kernel(
+    members, tok_ref, cot_ref, len_ref, tok_out, cot_out, len_out,
+    local_sem, send_sem, recv_sem, len_send, len_recv,
+):
+    dp = lax.axis_index("dp")
+    tensor = lax.axis_index("tensor")
+    base = dp // GROUP * GROUP
+    own = dp % GROUP
+    barrier = pltpu.get_barrier_semaphore()
+
+    def greet(step, carry):
+        signal(barrier, (dp + step) % members, tensor)
+        return carry
+
+    lax.fori_loop(1, members, greet, 0)
+    local = [
+        pltpu.make_async_copy(source.at[:, :, 0], target.at[0], local_sem.at[i])
+        for i, (source, target) in enumerate(((tok_ref, tok_out), (cot_ref, cot_out)))
+    ]
+    for copy in local:
+        copy.start()
+    keep = pltpu.make_async_copy(len_ref, len_out.at[dp], local_sem.at[2])
+    keep.start()
+    pl.semaphore_wait(barrier, members - 1)
+
+    def len_copy(step):
+        return remote(
+            len_ref, len_out.at[dp], len_send.at[step - 1], len_recv.at[step - 1],
+            (dp + step) % members, tensor,
+        )
+
+    def share(step, carry):
+        len_copy(step).start()
+        return carry
+
+    lax.fori_loop(1, members, share, 0)
+    copies = []
+    for i, (source, target) in enumerate(((tok_ref, tok_out), (cot_ref, cot_out))):
+        for k in range(1, GROUP):
+            copies.append(
+                remote(
+                    source.at[:, :, k], target.at[k], send_sem.at[i, k], recv_sem.at[i, k],
+                    base + (own + k) % GROUP, tensor,
+                )
+            )
+    for copy in copies:
+        copy.start()
+
+    def collect(step, carry):
+        len_copy(step).wait()
+        return carry
+
+    lax.fori_loop(1, members, collect, 0)
+    for copy in local:
+        copy.wait()
+    keep.wait()
+    for copy in copies:
+        copy.wait()
+
+
+def exchange(tokens, cotangent, lengths, members):
+    seqs = lengths.shape[0]
+    rows, width = tokens.shape
+    rounds = rows // (seqs * GROUP * TILE)
+    shape = (seqs, rounds, GROUP, TILE, width)
+    slots = jax.ShapeDtypeStruct((GROUP, seqs, rounds, TILE, width), tokens.dtype)
+    padded = jnp.pad(lengths, (0, 128 - seqs)).reshape(1, 128)
+    anywhere = pl.BlockSpec(memory_space=pl.ANY)
+    tok, cot, lens = pl.pallas_call(
+        functools.partial(exchange_kernel, members),
+        out_shape=(slots, slots, jax.ShapeDtypeStruct((members, 1, 128), jnp.int32)),
+        in_specs=[anywhere, anywhere, pl.BlockSpec(memory_space=pltpu.VMEM)],
+        out_specs=(anywhere, anywhere, pl.BlockSpec(memory_space=pltpu.VMEM)),
+        scratch_shapes=[
+            pltpu.SemaphoreType.DMA((3,)),
+            pltpu.SemaphoreType.DMA((2, GROUP)),
+            pltpu.SemaphoreType.DMA((2, GROUP)),
+            pltpu.SemaphoreType.DMA((members - 1,)),
+            pltpu.SemaphoreType.DMA((members - 1,)),
+        ],
+        compiler_params=pltpu.CompilerParams(collective_id=0, has_side_effects=True),
+        name="exchange",
+    )(tokens.reshape(shape), cotangent.reshape(shape), padded)
+    return tok.reshape(rows, width), cot.reshape(rows, width), lens[:, 0, :seqs]
+
+
+def tile_count(length, k):
+    cycle = GROUP * TILE
+    return length // cycle * TILE + jnp.clip(length % cycle - TILE * k, 0, TILE)
+
+
+def layer_kernel(
+    cap, seqs, rounds,
+    lens_ref, tok_slots, cot_slots, gain_ref, wg_ref, wu_ref, wd_ref,
+    layer_ref, grad_ref,
+    wgu, wd, tokf, cotf, hidden, act, dact, both, ggug, scale_ref, mean_ref,
+    layer_send, layer_recv, grad_send, grad_recv, layer_back, grad_back,
+    w_sem, ag_send, ag_recv, rs_send, rs_recv, out_send, out_recv,
+):
+    f32, bf16 = jnp.float32, jnp.bfloat16
+    dp = lax.axis_index("dp")
+    tensor = lax.axis_index("tensor")
+    base = dp // GROUP * GROUP
+    own = dp % GROUP
+    width = tok_slots.shape[1]
+    parts = tokf.shape[1] // width
+    units = hidden.shape[1]
+    seg = rounds * TILE
+
+    pieces = units // 128
+    w_copies = []
+    for j in range(pieces):
+        for i, source in enumerate((wg_ref, wu_ref)):
+            w_copies.append(
+                pltpu.make_async_copy(
+                    source.at[:, pl.ds(j * 128, 128)],
+                    wgu.at[:, pl.ds(j * 256 + i * 128, 128)],
+                    w_sem.at[2 * j + i],
+                )
+            )
+    w_copies.append(pltpu.make_async_copy(wd_ref, wd, w_sem.at[2 * pieces]))
+    for copy in w_copies:
+        copy.start()
+    barrier = pltpu.get_barrier_semaphore()
+    for k in range(1, parts):
+        signal(barrier, dp, tensor ^ k)
+    for k in range(1, GROUP):
+        signal(barrier, base + (own + k) % GROUP, tensor)
+
+    counts, starts, total = [], [], jnp.int32(0)
+    for k in range(GROUP):
+        home = base + (own - k + GROUP) % GROUP
+        for s in range(seqs):
+            count = tile_count(lens_ref[home * seqs + s], k)
+            counts.append(count)
+            starts.append(total)
+            total = total + count
+    slot_rows = GROUP * seqs * seg
+    lane = lax.broadcasted_iota(jnp.int32, (1, slot_rows), 1)
+    place = jnp.full((1, slot_rows), -1, jnp.int32)
+    for i in range(GROUP * seqs):
+        inside = lane - i * seg
+        place = jnp.where((inside >= 0) & (inside < counts[i]), inside + starts[i], place)
+    row = lax.broadcasted_iota(jnp.int32, (cap, slot_rows), 0)
+    picks = jnp.where(row == place, 1.0, 0.0).astype(bf16)
+    block = pl.ds(pl.multiple_of(tensor * width, width), width)
+    tokf[:, block] = jnp.dot(picks, tok_slots[...], preferred_element_type=f32).astype(bf16)
+    cotf[:, block] = jnp.dot(picks, cot_slots[...], preferred_element_type=f32).astype(bf16)
+    pl.semaphore_wait(barrier, parts + GROUP - 2)
+
+    gathers = []
+    for i, full in enumerate((tokf, cotf)):
+        mine = []
+        for k in range(1, parts):
+            mine.append(
+                remote(
+                    full.at[:, block], full.at[:, block], ag_send.at[i, k], ag_recv.at[i, k],
+                    dp, tensor ^ k,
+                )
+            )
+        for copy in mine:
+            copy.start()
+        gathers.append(mine)
+    for copy in gathers[0]:
+        copy.wait_recv()
+
+    def square(b, total):
+        x = tokf[:, pl.ds(pl.multiple_of(b * width, width), width)].astype(f32)
+        return total + jnp.sum(x * x, axis=1, keepdims=True)
+
+    total_sq = lax.fori_loop(0, parts, square, jnp.zeros((cap, 1), f32))
+    scaler = lax.rsqrt(total_sq * (1.0 / (parts * width)) + EPSILON)
+    scale_ref[...] = jnp.broadcast_to(scaler, (cap, 128))
+    normed = ggug
+
+    def norm(b, carry):
+        at = pl.ds(pl.multiple_of(b * width, width), width)
+        x = tokf[:, at].astype(f32)
+        normed[:, at] = (x * scale_ref[:, :1] * gain_ref[:, at].astype(f32)).astype(bf16)
+        return carry
+
+    lax.fori_loop(0, parts, norm, 0)
+    for copy in w_copies:
+        copy.wait()
+
+    def forward(j, carry):
+        at = pl.ds(pl.multiple_of(j * 128, 128), 128)
+        gu = jnp.dot(
+            normed[:, : parts * width], wgu[:, pl.ds(pl.multiple_of(j * 256, 256), 256)],
+            preferred_element_type=f32,
+        )
+        gate, up = gu[:, :128], gu[:, 128:]
+        sigmoid = jax.nn.sigmoid(gate)
+        silu = gate * sigmoid
+        slope = up * sigmoid * (1.0 + gate * (1.0 - sigmoid))
+        hidden[:, at] = (silu * up).astype(bf16)
+        act[:, at] = silu
+        dact[:, at] = slope
+        both[:, at] = slope * gate + silu * up
+        return carry
+
+    lax.fori_loop(0, pieces, forward, 0)
+
+    def layer_part(k):
+        at = pl.ds(pl.multiple_of((tensor ^ k) * width, width), width)
+        return jnp.dot(hidden[...], wd[:, at], preferred_element_type=f32).astype(bf16)
+
+    def rs_copy(i, k, send, recv):
+        return remote(
+            send.at[k], recv.at[k], rs_send.at[i, k], rs_recv.at[i, k], dp, tensor ^ k
+        )
+
+    def layer_step(k, carry):
+        layer_send[k] = layer_part(k)
+        rs_copy(0, k, layer_send, layer_recv).start()
+        return carry
+
+    lax.fori_loop(1, parts, layer_step, 0)
+    layer_send[0] = layer_part(0)
+
+    for copy in gathers[1]:
+        copy.wait_recv()
+
+    mean_ref[...] = jnp.zeros_like(mean_ref)
+
+    def backward(j, carry):
+        at = pl.ds(pl.multiple_of(j * 128, 128), 128)
+        hgrad = lax.dot_general(cotf[...], wd[at, :], NT, preferred_element_type=f32)
+        ggug[:, pl.ds(pl.multiple_of(j * 256, 256), 128)] = (hgrad * dact[:, at]).astype(bf16)
+        ggug[:, pl.ds(pl.multiple_of(j * 256 + 128, 128), 128)] = (hgrad * act[:, at]).astype(bf16)
+        mean_ref[...] += hgrad * both[:, at]
+        return carry
+
+    lax.fori_loop(0, pieces, backward, 0)
+    mean = jnp.sum(mean_ref[...], axis=1, keepdims=True) * (1.0 / (parts * width))
+    mean_ref[...] = jnp.broadcast_to(mean * scale_ref[:, :1], (cap, 128))
+
+    def grad_part(k):
+        at = pl.ds(pl.multiple_of((tensor ^ k) * width, width), width)
+        terms = lax.dot_general(
+            ggug[:, : 2 * units], wgu[at, :], NT, preferred_element_type=f32
+        )
+        unit_part = tokf[:, at].astype(f32) * mean_ref[:, :1]
+        return (scale_ref[:, :1] * (terms * gain_ref[:, at].astype(f32) - unit_part)).astype(bf16)
+
+    def grad_step(k, carry):
+        grad_send[k] = grad_part(k)
+        rs_copy(1, k, grad_send, grad_recv).start()
+        return carry
+
+    lax.fori_loop(1, parts, grad_step, 0)
+    grad_send[0] = grad_part(0)
+
+    def finish(i, full, send, recv, back, out):
+        for k in range(1, parts):
+            rs_copy(i, k, send, recv).wait_recv()
+        result = full[:, block].astype(f32) + send[0].astype(f32)
+        for k in range(1, parts):
+            result = result + recv[k].astype(f32)
+        result = result.astype(bf16)
+        copies = []
+        for k in list(range(1, GROUP)) + [0]:
+            inside = lax.broadcasted_iota(jnp.int32, (seqs * seg, 1), 0)
+            here = jnp.full((seqs * seg, 1), -1, jnp.int32)
+            for s in range(seqs):
+                at = inside - s * seg
+                here = jnp.where(
+                    (at >= 0) & (at < counts[k * seqs + s]), at + starts[k * seqs + s], here
+                )
+            column = lax.broadcasted_iota(jnp.int32, (seqs * seg, cap), 1)
+            spread = jnp.where(column == here, 1.0, 0.0).astype(bf16)
+            rows = jnp.dot(spread, result, preferred_element_type=f32)
+            back[k] = rows.reshape(seqs, rounds, TILE, width).astype(bf16)
+            if k:
+                copy = remote(
+                    back.at[k], out.at[:, :, k], out_send.at[i, k], out_recv.at[i, k],
+                    base + (own - k + GROUP) % GROUP, tensor,
+                )
+            else:
+                copy = pltpu.make_async_copy(back.at[0], out.at[:, :, 0], out_send.at[i, 0])
+            copy.start()
+            copies.append(copy)
+        return copies
+
+    copies = finish(0, tokf, layer_send, layer_recv, layer_back, layer_ref)
+    copies += finish(1, cotf, grad_send, grad_recv, grad_back, grad_ref)
+    for mine in gathers:
+        for copy in mine:
+            copy.wait_send()
+    for i, (send, recv) in enumerate(((layer_send, layer_recv), (grad_send, grad_recv))):
+        for k in range(1, parts):
+            rs_copy(i, k, send, recv).wait_send()
+    for copy in copies:
+        copy.wait()
+
+
+def layer(cap, number, lens, tok, cot, gain, gate_weight, up_weight, down_weight):
+    rows, width = tok.shape
+    units, features = down_weight.shape
+    parts = features // width
+    seqs = lens.shape[1]
+    rounds = rows // (seqs * GROUP * TILE)
+    f32, bf16 = jnp.float32, jnp.bfloat16
+    out = jax.ShapeDtypeStruct((seqs, rounds, GROUP, TILE, width), bf16)
+    anywhere = pl.BlockSpec(memory_space=pl.ANY)
+    vmem = pl.BlockSpec(memory_space=pltpu.VMEM)
+    exchange_buffer = pltpu.VMEM((parts, cap, width), bf16)
+    back_buffer = pltpu.VMEM((GROUP, seqs, rounds, TILE, width), bf16)
+    layer_out, input_grad = pl.pallas_call(
+        functools.partial(layer_kernel, cap, seqs, rounds),
+        out_shape=(out, out),
+        in_specs=[pl.BlockSpec(memory_space=pltpu.SMEM), vmem, vmem, vmem]
+        + [anywhere] * 3,
+        out_specs=(anywhere, anywhere),
+        scratch_shapes=[
+            pltpu.VMEM((features, 2 * units), bf16),
+            pltpu.VMEM((units, features), bf16),
+            pltpu.VMEM((cap, features), bf16),
+            pltpu.VMEM((cap, features), bf16),
+            pltpu.VMEM((cap, units), bf16),
+            pltpu.VMEM((cap, units), f32),
+            pltpu.VMEM((cap, units), f32),
+            pltpu.VMEM((cap, units), f32),
+            pltpu.VMEM((cap, max(features, 2 * units)), bf16),
+            pltpu.VMEM((cap, 128), f32),
+            pltpu.VMEM((cap, 128), f32),
+            exchange_buffer, exchange_buffer, exchange_buffer, exchange_buffer,
+            back_buffer, back_buffer,
+            pltpu.SemaphoreType.DMA((2 * (units // 128) + 1,)),
+            pltpu.SemaphoreType.DMA((2, parts)),
+            pltpu.SemaphoreType.DMA((2, parts)),
+            pltpu.SemaphoreType.DMA((2, parts)),
+            pltpu.SemaphoreType.DMA((2, parts)),
+            pltpu.SemaphoreType.DMA((2, GROUP)),
+            pltpu.SemaphoreType.DMA((2, GROUP)),
+        ],
+        compiler_params=pltpu.CompilerParams(
+            collective_id=number, has_side_effects=True, vmem_limit_bytes=58 << 20
+        ),
+        name=f"layer_{cap}",
+    )(lens.reshape(-1), tok, cot, gain.reshape(1, -1), gate_weight, up_weight, down_weight)
+    return layer_out.reshape(rows, width), input_grad.reshape(rows, width)
+
+
+def largest_load(lens):
+    planes = lens.reshape(-1, GROUP, lens.shape[1])
+    member = jnp.arange(GROUP, dtype=jnp.int32)
+    phase = (member[:, None] - member[None, :]) % GROUP
+    count = tile_count(planes[:, None], phase[None, :, :, None])
+    return jnp.max(jnp.sum(count, axis=(2, 3)))
+
+
+def shards(tokens, gain, gate_weight, up_weight, down_weight, cotangent, lengths):
+    members = lax.axis_size("dp")
+    tok, cot, lens = exchange(tokens, cotangent, lengths, members)
+    load = largest_load(lens)
+    choice = jnp.sum((load > jnp.array(CAPACITIES, jnp.int32)).astype(jnp.int32))
+
+    def sized(number, cap):
+        return lambda: layer(
+            cap, number, lens, tok, cot, gain, gate_weight, up_weight, down_weight
+        )
+
+    branches = [sized(i + 1, cap) for i, cap in enumerate(CAPACITIES)]
+    branches.append(
+        lambda: spread_evenly(
+            tokens, gain, gate_weight, up_weight, down_weight, cotangent, lengths
+        )
+    )
+    return lax.switch(choice, branches)
 
 
 def lookup_small(index_values, table):
@@ -64,7 +454,7 @@
     return (layer_part, grad_part)
 
 
-def shards(tokens, gain, gate_weight, up_weight, down_weight, cotangent, lengths):
+def spread_evenly(tokens, gain, gate_weight, up_weight, down_weight, cotangent, lengths):
     row_total, width_part = tokens.shape
     seq_count = lengths.shape[0]
     seq_length = row_total // seq_count

time: 375 us -> 133 us (0.35)
  waiting for transfers between devices: 216 us -> 0 us
  Pallas kernels: 0 us -> 107 us
  blocking collectives: 45.5 us -> 0 us
  starting transfers between devices: 32.6 us -> 0 us
  local copies, waits for them, and re-layouts: 25.7 us -> 6.92 us
  other arithmetic: 20.8 us -> 2.76 us
  matrix products: 16.5 us -> 0 us
    pallas_call x0 -> x2, Pallas kernels: none -> 107 us  [the longest x1 80.4 us: layer(): pl.pallas_call(functools.partial(layer_kernel, cap, seqs, rounds), out_sh...]
    psum x1 -> x0, waiting for transfers between devices: 82.7 us -> none  [layer_core(): normed_grad = lax.psum(normed_terms, 'tensor')]
    all_gather x2 -> x0, waiting for transfers between devices: 65.5 us -> none  [the longest x1 33 us: layer_core(): lax.all_gather(cotan_part, 'tensor', axis=1, tiled=True)]
    reduce_scatter x1 -> x0, waiting for transfers between devices: 35.2 us -> none  [layer_core(): lax.psum_scatter(layer_terms.astype(jnp.bfloat16), 'tensor', scatter_dime...]
    all_to_all x3 -> x0, starting transfers between devices: 32.2 us -> none  [the longest x1 14.2 us: shards(): lax.all_to_all(unpack_slots(layer_packed), 'dp', split_axis=0, concat_axi...]
    all_to_all x3 -> x0, waiting for transfers between devices: 31.5 us -> none  [the longest x1 18.1 us: shards(): lax.all_to_all(pack_rows(tokens), 'dp', split_axis=0, concat_axis=0, tile...]
    all_to_all x1 -> x0, blocking collectives: 26.9 us -> none  [shards(): lax.all_to_all(pack_rows(cotangent), 'dp', split_axis=0, concat_axis=0, t...]
    unnamed x1 -> x0, blocking collectives: 18.6 us -> none
  transfers between devices with their start and end apart: 7 -> 0, of which waited for: 6 -> 0; matrix products, arithmetic and copies ran while one was open for 9% -> 0% of each run, Pallas kernels for 0% -> 0%
where the time goes in v1:
time: 133 us; the launch traced here: 131 us
  Pallas kernels  107 us (80%)
  between operations  14.7 us (11%)
  local copies, waits for them, and re-layouts  6.92 us (5%)
  other arithmetic  2.76 us (2%)
    pallas_call x1, Pallas kernels, layer(): pl.pallas_call(functools.partial(layer_kernel, cap, seqs, rounds), out_sh...  80.4 us
    pallas_call x1, Pallas kernels, exchange(): pl.pallas_call(functools.partial(exchange_kernel, members), out_shape=(sl...  26.2 us
    unnamed x2, local copies, waits for them, and re-layouts  3.74 us

profile of v1, /device:TPU:1, one launch (start us, length us, event | category | flops | bytes accessed | tf_op | source)
XLA Modules:
  0.0 131.4 jit_solution(18416033378403213124)
XLA Ops:
  7.2 1.2 pad_bitcast_fusion.len_ref
  8.3 26.2 %exchange.1 = (bf16[8,2,8,8,256]{4,3,2,1,0:T(8,128)(2,1)S(1)}, bf16[8,2,8,8,256]{4,3,2,1,0:T(8,128)(2,1)S(1)}, s32[32,1,128]{2,1,0:T(1,128)S(1)}) custom-call(bf16[2,8,8,8,256]{4,3,2,1,0:T(8,128)(2,1)} %bitcast.59, bf16[2,8,8,8,256]{4,3,2,1,0:T(8,128)(2,1)} %bitcast.60, s32[1,128]{1,0:T(1,128)} %pad_bitcast_fusion.len_ref), custom_call_target="tpu_custom_call" | custom-call | tf_op jit(solution)/shard_map/exchange/pallas_call | solution.py:98
  34.5 0.1 copy.49
  34.7 0.2 add_reduce_fusion
  34.8 0.6 reduce_max.9
  35.4 1.9 %fusion.47 = s32[]{:T(128)} fusion(s32[5]{0:T(128)} %constant.199.clone, s32[]{:T(128)} %reduce_max.9), kind=kLoop, calls=%fused_computation.134 | loop fusion | flops 14 | bytes 28 | tf_op jit(solution)/shard_map/reduce_sum | solution.py:386
  38.0 82.8 %conditional.1 = (bf16[1024,256]{1,0:T(8,128)(2,1)}, bf16[1024,256]{1,0:T(8,128)(2,1)}) conditional(s32[]{:T(128)} %clamp.4, (s32[32,1,2]{2,1,0:T(1,128)S(1)}, bf16[8,2,8,8,256]{4,3,2,1,0:T(8,128)(2,1)S(1)}, bf16[8,2,8,8,256]{4,3,2,1,0:T(8,128)(2,1)S(1)}, bf16[2048]{0:T(1024)(128)(2,1)}, bf16[2048,896]{1,0:T(8,128)(2,1)}, ...), branch_computations={%region_3.4_spmd, %region_4.5_spmd, %region_5.6_spmd, %region_6.7_... | conditional | flops 5655228416 | bytes 168585616 | solution.py:399
  38.1 0.6 reshape_squeeze.10.lens_ref
  38.7 1.3 reshape.435.gain_ref
  40.0 80.4 %layer_320.1 = (bf16[2,8,8,8,256]{4,3,2,1,0:T(8,128)(2,1)}, bf16[2,8,8,8,256]{4,3,2,1,0:T(8,128)(2,1)}) custom-call(s32[64]{0:T(128)} %reshape_squeeze.10.lens_ref, bf16[1024,256]{1,0:T(8,128)(2,1)S(1)} %bitcast.61, bf16[1024,256]{1,0:T(8,128)(2,1)S(1)} %bitcast.66, bf16[1,2048]{1,0:T(2,128)(2,1)} %reshape.435.gain_ref, ...), custom_call_target="tpu_custom_call" | custom-call | tf_op jit(solution)/shard_map/cond/branch_0_fun/layer_320/pallas_call | solution.py:338
  120.9 1.9 %copy.66 = bf16[1024,256]{1,0:T(8,128)(2,1)} copy(bf16[1024,256]{1,0:T(8,128)(2,1)} %get-tuple-element.306) | data formatting | bytes 1048576
  122.7 1.9 %copy.67 = bf16[1024,256]{1,0:T(8,128)(2,1)} copy(bf16[1024,256]{1,0:T(8,128)(2,1)} %get-tuple-element.307) | data formatting | bytes 1048576
  (4 shorter events, 0.0 us)

commit v2 on v0

v2 whole, which is shorter than its diff:
```python
import functools

import jax
import jax.numpy as jnp
from jax import lax
from jax.experimental import pallas as pl
from jax.experimental.pallas import tpu as pltpu
from jax.sharding import PartitionSpec as P

EPSILON = 1e-05
GROUP = 8
TILE = 8
CAPACITIES = (320, 352, 384, 448, 1024)
MESH = pl.DeviceIdType.MESH
NT = (((1,), (1,)), ((), ()))
f32, bf16, i32 = jnp.float32, jnp.bfloat16, jnp.int32


def remote(src, dst, send_sem, recv_sem, dp, tensor):
    return pltpu.make_async_remote_copy(
        src_ref=src, dst_ref=dst, send_sem=send_sem, recv_sem=recv_sem,
        device_id=(dp, tensor), device_id_type=MESH,
    )


def signal(sem, dp, tensor):
    pl.semaphore_signal(sem, inc=1, device_id=(dp, tensor), device_id_type=MESH)


def tile_count(length, k):
    cycle = GROUP * TILE
    return length // cycle * TILE + jnp.clip(length % cycle - TILE * k, 0, TILE)


def exchange_kernel(
    members, tok_ref, info_ref, tok_out, info_out, choice_ref,
    local_sem, send_sem, recv_sem, info_send, info_recv,
):
    dp = lax.axis_index("dp")
    tensor = lax.axis_index("tensor")
    base = dp // GROUP * GROUP
    own = dp % GROUP
    barrier = pltpu.get_barrier_semaphore()

    def greet(step, carry):
        signal(barrier, (dp + step) % members, tensor)
        return carry

    lax.fori_loop(1, members, greet, 0)
    local = pltpu.make_async_copy(tok_ref.at[:, :, 0], tok_out.at[0], local_sem.at[0])
    local.start()
    info_out[dp] = info_ref[...]
    pl.semaphore_wait(barrier, members - 1)

    def info_copy(step):
        return remote(
            info_ref, info_out.at[dp], info_send.at[step - 1], info_recv.at[step - 1],
            (dp + step) % members, tensor,
        )

    def share(step, carry):
        info_copy(step).start()
        return carry

    copies = [
        remote(
            tok_ref.at[:, :, k], tok_out.at[k], send_sem.at[k], recv_sem.at[k],
            base + (own + k) % GROUP, tensor,
        )
        for k in range(1, GROUP)
    ]
    for copy in copies:
        copy.start()
    lax.fori_loop(1, members, share, 0)

    def collect(step, carry):
        info_copy(step).wait()
        return carry

    lax.fori_loop(1, members, collect, 0)
    load = jnp.zeros((1, 128), i32)
    for plane in range(members // GROUP):
        held = info_out[plane * GROUP]
        for h in range(1, GROUP):
            held = held + info_out[plane * GROUP + h]
        load = jnp.maximum(load, held)
    lane = lax.broadcasted_iota(i32, (1, 128), 1)
    most = jnp.max(jnp.where(lane < GROUP, load, 0))
    choice = jnp.int32(0)
    for cap in CAPACITIES[:-1]:
        choice = choice + (most > cap).astype(i32)
    choice_ref[0] = choice
    local.wait()
    for copy in copies:
        copy.wait()


def exchange(tokens, lengths, members):
    seqs = lengths.shape[0]
    rows, width = tokens.shape
    rounds = rows // (seqs * GROUP * TILE)
    slots = jax.ShapeDtypeStruct((GROUP, seqs, rounds, TILE, width), tokens.dtype)
    lane = jnp.arange(128, dtype=i32)
    phase = (lane - lax.axis_index("dp")) % GROUP
    info = jnp.where(lane < GROUP, jnp.sum(tile_count(lengths[:, None], phase), axis=0), 0)
    for s in range(seqs):
        info = jnp.where(lane == GROUP + s, lengths[s], info)
    anywhere = pl.BlockSpec(memory_space=pl.ANY)
    vmem = pl.BlockSpec(memory_space=pltpu.VMEM)
    tok, shared, choice = pl.pallas_call(
        functools.partial(exchange_kernel, members),
        out_shape=(
            slots, jax.ShapeDtypeStruct((members, 1, 128), i32), jax.ShapeDtypeStruct((1,), i32)
        ),
        in_specs=[anywhere, vmem],
        out_specs=(anywhere, vmem, pl.BlockSpec(memory_space=pltpu.SMEM)),
        scratch_shapes=[
            pltpu.SemaphoreType.DMA((1,)),
            pltpu.SemaphoreType.DMA((GROUP,)),
            pltpu.SemaphoreType.DMA((GROUP,)),
            pltpu.SemaphoreType.DMA((members - 1,)),
            pltpu.SemaphoreType.DMA((members - 1,)),
        ],
        compiler_params=pltpu.CompilerParams(collective_id=0, has_side_effects=True),
        name="exchange",
    )(tokens.reshape(seqs, rounds, GROUP, TILE, width), info.reshape(1, 128))
    return tok.reshape(rows, width), shared, choice[0]


def layer_kernel(
    cap, split, seqs, rounds,
    info_ref, tok_slots, gain_ref, cot_ref, wg_ref, wu_ref, wd_ref,
    layer_ref, grad_ref,
    wgu, wd, cot_slots, tokf, cotf, hidden, act, dact, both, ggug, scale_ref, mean_ref,
    layer_send, layer_recv, grad_send, grad_recv, layer_back, grad_back,
    w_sem, in_send, in_recv, ag_send, ag_recv, rs_send, rs_recv, out_send, out_recv,
):
    dp = lax.axis_index("dp")
    tensor = lax.axis_index("tensor")
    base = dp // GROUP * GROUP
    own = dp % GROUP
    width = tok_slots.shape[1]
    parts = tokf.shape[1] // width
    units = hidden.shape[1]
    seg = rounds * TILE
    early, late = pl.ds(0, split), pl.ds(split, cap - split)

    pieces = units // 128
    w_copies = []
    for j in range(pieces):
        for i, source in enumerate((wg_ref, wu_ref)):
            w_copies.append(
                pltpu.make_async_copy(
                    source.at[:, pl.ds(j * 128, 128)],
                    wgu.at[:, pl.ds(j * 256 + i * 128, 128)],
                    w_sem.at[2 * j + i],
                )
            )
    w_copies.append(pltpu.make_async_copy(wd_ref, wd, w_sem.at[2 * pieces]))
    barrier = pltpu.get_barrier_semaphore()
    for k in range(1, 5):
        signal(barrier, dp, tensor ^ k)
    for k in range(1, GROUP):
        signal(barrier, base + (own + k) % GROUP, tensor)
    cot_in = [pltpu.make_async_copy(cot_ref.at[:, :, 0], cot_slots.at[0], in_send.at[0])]
    for k in range(1, GROUP):
        cot_in.append(
            remote(
                cot_ref.at[:, :, k], cot_slots.at[k], in_send.at[k], in_recv.at[k],
                base + (own + k) % GROUP, tensor,
            )
        )
    cot_in[0].start()

    counts, starts, total = [], [], jnp.int32(0)
    for k in range(GROUP):
        home = base + (own - k + GROUP) % GROUP
        for s in range(seqs):
            count = tile_count(info_ref[home, 0, GROUP + s], k)
            counts.append(count)
            starts.append(total)
            total = total + count
    slot_rows = GROUP * seqs * seg
    lane = lax.broadcasted_iota(i32, (1, slot_rows), 1)
    place = jnp.full((1, slot_rows), -1, i32)
    for i in range(GROUP * seqs):
        inside = lane - i * seg
        place = jnp.where((inside >= 0) & (inside < counts[i]), inside + starts[i], place)

    def compact(slots):
        row = lax.broadcasted_iota(i32, (cap, slot_rows), 0)
        picks = jnp.where(row == place, 1.0, 0.0).astype(bf16)
        return jnp.dot(picks, slots, preferred_element_type=f32).astype(bf16)

    def at(k):
        return pl.ds(pl.multiple_of((tensor ^ k) * width, width), width)

    tokf[:, at(0)] = compact(tok_slots[...])
    pl.semaphore_wait(barrier, 4 + GROUP - 1)

    def first_hop(i, full):
        return [
            remote(
                full.at[:, at(0)], full.at[:, at(0)], ag_send.at[i, k], ag_recv.at[i, k],
                dp, tensor ^ k,
            )
            for k in (4, 1, 3, 2)
        ]

    def second_hop(i, full):
        to_y = [
            remote(
                full.at[early, at(4)], full.at[early, at(4)],
                ag_send.at[i, 4 + k], ag_recv.at[i, 4 + k], dp, tensor ^ k,
            )
            for k in (1, 3, 2)
        ]
        to_z = [
            remote(
                full.at[late, at(k)], full.at[late, at(k)],
                ag_send.at[i, 7 + k], ag_recv.at[i, 7 + k], dp, tensor ^ 4,
            )
            for k in (1, 3, 2)
        ]
        return to_y, to_z

    def pass_on(first, second):
        to_y, to_z = second
        first[0].wait_recv()
        for copy in to_y:
            copy.start()
        for arrived, copy in zip(first[1:], to_z):
            arrived.wait_recv()
            copy.start()

    tok_first, tok_second = first_hop(0, tokf), second_hop(0, tokf)
    cot_first, cot_second = first_hop(1, cotf), second_hop(1, cotf)
    for copy in tok_first:
        copy.start()
    for copy in cot_in[1:]:
        copy.start()
    for copy in w_copies:
        copy.start()
    pass_on(tok_first, tok_second)
    cot_in[0].wait()
    for copy in cot_in[1:]:
        copy.wait_recv()
    cotf[:, at(0)] = compact(cot_slots[...].reshape(slot_rows, width))
    for copy in tok_second[0] + tok_second[1]:
        copy.wait_recv()
    for copy in cot_first:
        copy.start()

    def square(b, total):
        x = tokf[:, pl.ds(pl.multiple_of(b * width, width), width)].astype(f32)
        return total + jnp.sum(x * x, axis=1, keepdims=True)

    total_sq = lax.fori_loop(0, parts, square, jnp.zeros((cap, 1), f32))
    scaler = lax.rsqrt(total_sq * (1.0 / (parts * width)) + EPSILON)
    scale_ref[...] = jnp.broadcast_to(scaler, (cap, 128))
    normed = ggug

    def norm(b, carry):
        here = pl.ds(pl.multiple_of(b * width, width), width)
        x = tokf[:, here].astype(f32)
        normed[:, here] = (x * scale_ref[:, :1] * gain_ref[:, here].astype(f32)).astype(bf16)
        return carry

    lax.fori_loop(0, parts, norm, 0)
    for copy in w_copies:
        copy.wait()

    def forward(j, carry):
        here = pl.ds(pl.multiple_of(j * 128, 128), 128)
        gu = jnp.dot(
            normed[:, : parts * width], wgu[:, pl.ds(pl.multiple_of(j * 256, 256), 256)],
            preferred_element_type=f32,
        )
        gate, up = gu[:, :128], gu[:, 128:]
        sigmoid = jax.nn.sigmoid(gate)
        silu = gate * sigmoid
        slope = up * sigmoid * (1.0 + gate * (1.0 - sigmoid))
        hidden[:, here] = (silu * up).astype(bf16)
        act[:, here] = silu
        dact[:, here] = slope
        both[:, here] = slope * gate + silu * up
        return carry

    lax.fori_loop(0, pieces, forward, 0)
    pass_on(cot_first, cot_second)

    def scatter_copy(i, send, recv, slot, rows, half, peer):
        return remote(
            send.at[slot, rows], recv.at[slot, rows],
            rs_send.at[i, half, slot], rs_recv.at[i, half, slot], dp, tensor ^ peer,
        )

    def scatter_first(i, send, recv, part):
        def far(k, carry):
            send[k] = part(k)
            scatter_copy(i, send, recv, k, late, 1, 4).start()

            @pl.when(k > 4)
            def _():
                scatter_copy(i, send, recv, k, early, 0, k - 4).start()

            return carry

        def near(k, carry):
            send[k] = part(k)
            scatter_copy(i, send, recv, k, early, 0, k).start()
            return carry

        lax.fori_loop(4, parts, far, 0)
        lax.fori_loop(1, 4, near, 0)
        send[0] = part(0)

    def scatter_second(i, send, recv):
        total = send[4, early].astype(f32)
        for k in (5, 6, 7):
            scatter_copy(i, send, recv, k, early, 0, k - 4).wait_recv()
            total = total + recv[k, early].astype(f32)
        send[4, early] = total.astype(bf16)
        scatter_copy(i, send, recv, 4, early, 0, 4).start()
        for k in (1, 2, 3):
            scatter_copy(i, send, recv, 4 + k, late, 1, 4).wait_recv()
            both_parts = send[k, late].astype(f32) + recv[4 + k, late].astype(f32)
            send[k, late] = both_parts.astype(bf16)
            scatter_copy(i, send, recv, k, late, 1, k).start()

    def scatter_rest(i, send, recv):
        rest = [scatter_copy(i, send, recv, k, early, 0, k) for k in (1, 2, 3)]
        rest.append(scatter_copy(i, send, recv, 4, late, 1, 4))
        rest.append(scatter_copy(i, send, recv, 4, early, 0, 4))
        rest += [scatter_copy(i, send, recv, k, late, 1, k) for k in (1, 2, 3)]
        return rest

    def layer_part(k):
        return jnp.dot(hidden[...], wd[:, at(k)], preferred_element_type=f32).astype(bf16)

    scatter_first(0, layer_send, layer_recv, layer_part)
    for copy in cot_second[0] + cot_second[1]:
        copy.wait_recv()

    mean_ref[...] = jnp.zeros_like(mean_ref)

    def backward(j, carry):
        here = pl.ds(pl.multiple_of(j * 128, 128), 128)
        hgrad = lax.dot_general(cotf[...], wd[here, :], NT, preferred_element_type=f32)
        ggug[:, pl.ds(pl.multiple_of(j * 256, 256), 128)] = (hgrad * dact[:, here]).astype(bf16)
        ggug[:, pl.ds(pl.multiple_of(j * 256 + 128, 128), 128)] = (
            hgrad * act[:, here]
        ).astype(bf16)
        mean_ref[...] += hgrad * both[:, here]
        return carry

    lax.fori_loop(0, pieces, backward, 0)
    mean = jnp.sum(mean_ref[...], axis=1, keepdims=True) * (1.0 / (parts * width))
    mean_ref[...] = jnp.broadcast_to(mean * scale_ref[:, :1], (cap, 128))
    scatter_second(0, layer_send, layer_recv)

    def grad_part(k):
        terms = lax.dot_general(
            ggug[:, : 2 * units], wgu[at(k), :], NT, preferred_element_type=f32
        )
        unit_part = tokf[:, at(k)].astype(f32) * mean_ref[:, :1]
        return (scale_ref[:, :1] * (terms * gain_ref[:, at(k)].astype(f32) - unit_part)).astype(
            bf16
        )

    scatter_first(1, grad_send, grad_recv, grad_part)

    def way_home(i, back, out, k):
        if k == 0:
            return pltpu.make_async_copy(back.at[0], out.at[:, :, 0], out_send.at[i, 0])
        return remote(
            back.at[k], out.at[:, :, k], out_send.at[i, k], out_recv.at[i, k],
            base + (own - k + GROUP) % GROUP, tensor,
        )

    def finish(i, full, send, recv, back, out):
        for copy in scatter_rest(i, send, recv):
            copy.wait_recv()
        result = full[:, at(0)].astype(f32) + send[0].astype(f32)
        for k in range(1, 5):
            result = result + recv[k].astype(f32)
        result = result.astype(bf16)
        for k in (4, 5, 3, 2, 6, 7, 1, 0):
            inside = lax.broadcasted_iota(i32, (seqs * seg, 1), 0)
            here = jnp.full((seqs * seg, 1), -1, i32)
            for s in range(seqs):
                pos = inside - s * seg
                n = k * seqs + s
                here = jnp.where((pos >= 0) & (pos < counts[n]), pos + starts[n], here)
            column = lax.broadcasted_iota(i32, (seqs * seg, cap), 1)
            spread = jnp.where(column == here, 1.0, 0.0).astype(bf16)
            rows = jnp.dot(spread, result, preferred_element_type=f32)
            back[k] = rows.reshape(seqs, rounds, TILE, width).astype(bf16)
            way_home(i, back, out, k).start()

    finish(0, tokf, layer_send, layer_recv, layer_back, layer_ref)
    scatter_second(1, grad_send, grad_recv)
    finish(1, cotf, grad_send, grad_recv, grad_back, grad_ref)

    for copy in cot_in[1:]:
        copy.wait_send()
    for copy in tok_first + tok_second[0] + tok_second[1] + cot_first + cot_second[0] + cot_second[1]:
        copy.wait_send()
    for i, (send, recv) in enumerate(((layer_send, layer_recv), (grad_send, grad_recv))):
        for copy in scatter_rest(i, send, recv):
            copy.wait_send()
        for k in (1, 2, 3):
            scatter_copy(i, send, recv, 4 + k, early, 0, k).wait_send()
            scatter_copy(i, send, recv, 4 + k, late, 1, 4).wait_send()
    for i, (back, out) in enumerate(((layer_back, layer_ref), (grad_back, grad_ref))):
        for k in range(GROUP):
            way_home(i, back, out, k).wait()


def layer(cap, number, info, tok, cotangent, gain, gate_weight, up_weight, down_weight, seqs):
    rows, width = tok.shape
    units, features = down_weight.shape
    parts = features // width
    rounds = rows // (seqs * GROUP * TILE)
    split = cap * 4 // 10 // 16 * 16
    tiled = (seqs, rounds, GROUP, TILE, width)
    slots = (GROUP, seqs, rounds, TILE, width)
    out = jax.ShapeDtypeStruct(tiled, bf16)
    anywhere = pl.BlockSpec(memory_space=pl.ANY)
    vmem = pl.BlockSpec(memory_space=pltpu.VMEM)
    peer_buffer = pltpu.VMEM((parts, cap, width), bf16)
    layer_out, input_grad = pl.pallas_call(
        functools.partial(layer_kernel, cap, split, seqs, rounds),
        out_shape=(out, out),
        in_specs=[pl.BlockSpec(memory_space=pltpu.SMEM), vmem, vmem] + [anywhere] * 4,
        out_specs=(anywhere, anywhere),
        scratch_shapes=[
            pltpu.VMEM((features, 2 * units), bf16),
            pltpu.VMEM((units, features), bf16),
            pltpu.VMEM(slots, bf16),
            pltpu.VMEM((cap, features), bf16),
            pltpu.VMEM((cap, features), bf16),
            pltpu.VMEM((cap, units), bf16),
            pltpu.VMEM((cap, units), f32),
            pltpu.VMEM((cap, units), f32),
            pltpu.VMEM((cap, units), f32),
            pltpu.VMEM((cap, max(features, 2 * units)), bf16),
            pltpu.VMEM((cap, 128), f32),
            pltpu.VMEM((cap, 128), f32),
            peer_buffer, peer_buffer, peer_buffer, peer_buffer,
            pltpu.VMEM(slots, bf16),
            pltpu.VMEM(slots, bf16),
            pltpu.SemaphoreType.DMA((2 * (units // 128) + 1,)),
            pltpu.SemaphoreType.DMA((GROUP,)),
            pltpu.SemaphoreType.DMA((GROUP,)),
            pltpu.SemaphoreType.DMA((2, 11)),
            pltpu.SemaphoreType.DMA((2, 11)),
            pltpu.SemaphoreType.DMA((2, 2, parts)),
            pltpu.SemaphoreType.DMA((2, 2, parts)),
            pltpu.SemaphoreType.DMA((2, GROUP)),
            pltpu.SemaphoreType.DMA((2, GROUP)),
        ],
        compiler_params=pltpu.CompilerParams(
            collective_id=number, has_side_effects=True, vmem_limit_bytes=62 << 20
        ),
        name=f"layer_{cap}",
    )(
        info, tok, gain.reshape(1, -1), cotangent.reshape(tiled),
        gate_weight, up_weight, down_weight,
    )
    return layer_out.reshape(rows, width), input_grad.reshape(rows, width)


def shards(tokens, gain, gate_weight, up_weight, down_weight, cotangent, lengths):
    tok, info, choice = exchange(tokens, lengths, lax.axis_size("dp"))

    def sized(number, cap):
        return lambda: layer(
            cap, number, info, tok, cotangent, gain, gate_weight, up_weight, down_weight,
            lengths.shape[0],
        )

    return lax.switch(choice, [sized(i + 1, cap) for i, cap in enumerate(CAPACITIES)])


def solution(mesh):
    placed = (
        P("dp", "tensor"),
        P(),
        P(None, "tensor"),
        P(None, "tensor"),
        P("tensor", None),
        P("dp", "tensor"),
        P("dp"),
    )
    return jax.shard_map(
        shards,
        mesh=mesh,
        in_specs=placed,
        out_specs=(P("dp", "tensor"), P("dp", "tensor")),
        check_vma=False,
    )
```

time: 375 us -> 91.7 us (0.24)
  waiting for transfers between devices: 216 us -> 0 us
  Pallas kernels: 0 us -> 82.6 us
  blocking collectives: 45.5 us -> 0 us
  starting transfers between devices: 32.6 us -> 0 us
  local copies, waits for them, and re-layouts: 25.7 us -> 4.19 us
  other arithmetic: 20.8 us -> 2.57 us
  matrix products: 16.5 us -> 0 us
  between operations: 16.7 us -> 1.34 us
    psum x1 -> x0, waiting for transfers between devices: 82.7 us -> none  [layer_core(): normed_grad = lax.psum(normed_terms, 'tensor')]
    pallas_call x0 -> x2, Pallas kernels: none -> 82.6 us  [the longest x1 61.8 us: layer(): pl.pallas_call(functools.partial(layer_kernel, cap, split, seqs, rounds),...]
    all_gather x2 -> x0, waiting for transfers between devices: 65.5 us -> none  [the longest x1 33 us: layer_core(): lax.all_gather(cotan_part, 'tensor', axis=1, tiled=True)]
    reduce_scatter x1 -> x0, waiting for transfers between devices: 35.2 us -> none  [layer_core(): lax.psum_scatter(layer_terms.astype(jnp.bfloat16), 'tensor', scatter_dime...]
    all_to_all x3 -> x0, starting transfers between devices: 32.2 us -> none  [the longest x1 14.2 us: shards(): lax.all_to_all(unpack_slots(layer_packed), 'dp', split_axis=0, concat_axi...]
    all_to_all x3 -> x0, waiting for transfers between devices: 31.5 us -> none  [the longest x1 18.1 us: shards(): lax.all_to_all(pack_rows(tokens), 'dp', split_axis=0, concat_axis=0, tile...]
    all_to_all x1 -> x0, blocking collectives: 26.9 us -> none  [shards(): lax.all_to_all(pack_rows(cotangent), 'dp', split_axis=0, concat_axis=0, t...]
    unnamed x1 -> x0, blocking collectives: 18.6 us -> none
  transfers between devices with their start and end apart: 7 -> 0, of which waited for: 6 -> 0; matrix products, arithmetic and copies ran while one was open for 9% -> 0% of each run, Pallas kernels for 0% -> 0%
where the time goes in v2:
time: 91.7 us; the launch traced here: 91.5 us
  Pallas kernels  82.6 us (90%)
  local copies, waits for them, and re-layouts  4.19 us (5%)
  other arithmetic  2.57 us (3%)
  between operations  1.34 us (1%)
    pallas_call x1, Pallas kernels, layer(): pl.pallas_call(functools.partial(layer_kernel, cap, split, seqs, rounds),...  61.8 us
    pallas_call x1, Pallas kernels, exchange(): pl.pallas_call(functools.partial(exchange_kernel, members), out_shape=(sl...  20.8 us

profile of v2, /device:TPU:1, one launch (start us, length us, event | category | flops | bytes accessed | tf_op | source)
XLA Modules:
  0.0 91.5 jit_solution(7069314614099674167)
XLA Ops:
  0.6 0.7 and_select_fusion.1
  1.3 0.1 add_reduce_fusion
  1.4 1.3 %fusion.3 = (s32[1]{0:T(128)}, s32[1]{0:T(128)}) fusion(s32[2]{0:T(128)} %param.18), kind=kLoop, calls=%fused_computation.15 | loop fusion | bytes 16 | tf_op jit(solution)/shard_map/slice | solution.py:107
  2.7 1.8 %compare_select_fusion.4.info_ref = s32[1,128]{1,0:T(1,128)} fusion(s32[128]{0:T(128)S(1)} %add_reduce_fusion, s32[]{:T(128)} %bitcast.7, s32[]{:T(128)} %bitcast.6), kind=kLoop, calls=%fused_computation.7 | loop fusion | flops 768 | bytes 1032 | tf_op jit(solution)/shard_map/jit(_where)/select_n | solution.py:107
  4.5 20.8 %exchange.1 = (bf16[8,2,8,8,256]{4,3,2,1,0:T(8,128)(2,1)S(1)}, s32[32,1,128]{2,1,0:T(1,128)S(1)}, s32[1]{0:T(128)}) custom-call(bf16[2,8,8,8,256]{4,3,2,1,0:T(8,128)(2,1)} %bitcast.24, s32[1,128]{1,0:T(1,128)} %compare_select_fusion.4.info_ref), custom_call_target="tpu_custom_call" | custom-call | tf_op jit(solution)/shard_map/exchange/pallas_call | solution.py:110
  26.0 63.9 %conditional.1 = ((bf16[2,8,8,8,256]{4,3,2,1,0:T(8,128)(2,1)S(1)}, bf16[2,8,8,8,256]{4,3,2,1,0:T(8,128)(2,1)S(1)})) conditional(s32[]{:T(128)} %bitcast.9, (bf16[2048]{0:T(1024)(128)(2,1)}, bf16[1024,256]{1,0:T(8,128)(2,1)}, s32[32,1,128]{2,1,0:T(1,128)S(1)}, bf16[1024,256]{1,0:T(8,128)(2,1)S(1)}, ...), branch_computations={%region_1.2_spmd, %region_2.3_spmd, %region_3.4_spmd, %region_4.5_... | conditional | bytes 8200 | solution.py:483
  26.0 1.3 %reshape.127.gain_ref = bf16[1,2048]{1,0:T(2,128)(2,1)} reshape(bf16[2048]{0:T(1024)(128)(2,1)} %get-tuple-element.72) | data formatting | bytes 8192 | tf_op jit(solution)/shard_map/cond/branch_0_fun/reshape | solution.py:468
  27.3 61.8 %layer_320.1 = (bf16[2,8,8,8,256]{4,3,2,1,0:T(8,128)(2,1)S(1)}, bf16[2,8,8,8,256]{4,3,2,1,0:T(8,128)(2,1)S(1)}) custom-call(s32[32,1,128]{2,1,0:T(1,128)S(1)} %get-tuple-element.70.info_ref, bf16[1024,256]{1,0:T(8,128)(2,1)S(1)} %get-tuple-element.71.tok_slots, bf16[1,2048]{1,0:T(2,128)(2,1)} %reshape.127.gain_ref, bf16[2,8,8,8,256]{4,3,2,1,0:T(8,128)(2,1)} %bitcast.14, ...), custom_call_target="tpu_custom_call" | custom-call | tf_op jit(solution)/shard_map/cond/branch_0_fun/layer_320/pallas_call | solution.py:432
  89.9 0.8 copy.21
  90.7 0.8 copy.22
  (1 shorter events, 0.0 us)

commit v3 on v0

v3 whole, which is shorter than its diff:
```python
import functools

import jax
import jax.numpy as jnp
from jax import lax
from jax.experimental import pallas as pl
from jax.experimental.pallas import tpu as pltpu
from jax.sharding import PartitionSpec as P

EPSILON = 1e-05
GROUP = 8
TILE = 8
CAPACITIES = (304, 336, 368, 416, 1024)
LARGE = 512
CHECK_AT = 3
MESH = pl.DeviceIdType.MESH
NT = (((1,), (1,)), ((), ()))
f32, bf16, i32 = jnp.float32, jnp.bfloat16, jnp.int32


def remote(src, dst, send_sem, recv_sem, dp, tensor):
    return pltpu.make_async_remote_copy(
        src_ref=src, dst_ref=dst, send_sem=send_sem, recv_sem=recv_sem,
        device_id=(dp, tensor), device_id_type=MESH,
    )


def signal(sem, dp, tensor):
    pl.semaphore_signal(sem, inc=1, device_id=(dp, tensor), device_id_type=MESH)


def tile_count(length, k):
    cycle = GROUP * TILE
    return length // cycle * TILE + jnp.clip(length % cycle - TILE * k, 0, TILE)


def exchange_kernel(
    planes, len_ref, tok_ref, tok_out, info_out, choice_ref,
    info, most, local_sem, send_sem, recv_sem, info_send, info_recv, most_send, most_recv,
):
    members = planes * GROUP
    dp = lax.axis_index("dp")
    tensor = lax.axis_index("tensor")
    plane = dp // GROUP
    base = plane * GROUP
    own = dp % GROUP
    seqs = len_ref.shape[0]
    barrier = pltpu.get_barrier_semaphore()

    def loop(low, high, step):
        def body(n, carry):
            step(n)
            return carry

        lax.fori_loop(low, high, body, 0)

    loop(1, GROUP, lambda k: signal(barrier, base + (own + k) % GROUP, tensor))
    loop(1, planes, lambda k: signal(barrier, (dp + k * GROUP) % members, tensor))
    local = pltpu.make_async_copy(tok_ref.at[:, :, 0], tok_out.at[0], local_sem.at[0])
    local.start()
    lane = lax.broadcasted_iota(i32, (1, 128), 1)
    phase = (lane + GROUP - own) % GROUP
    held = jnp.zeros((1, 128), i32)
    for s in range(seqs):
        held = held + tile_count(len_ref[s], phase)
    held = jnp.where(lane < GROUP, held, 0)
    for s in range(seqs):
        held = jnp.where(lane == GROUP + s, len_ref[s], held)
    info[...] = held
    info_out[own] = held
    pl.semaphore_wait(barrier, GROUP - 1 + planes - 1)

    def share(k):
        return remote(
            info, info_out.at[own], info_send.at[k], info_recv.at[k],
            base + (own + k) % GROUP, tensor,
        )

    def rows_to(k):
        return remote(
            tok_ref.at[:, :, k], tok_out.at[k], send_sem.at[k], recv_sem.at[k],
            base + (own + k) % GROUP, tensor,
        )

    def top(k):
        return remote(
            most.at[0], most.at[k], most_send.at[k], most_recv.at[k],
            (dp + k * GROUP) % members, tensor,
        )

    loop(1, GROUP, lambda k: share(k).start())
    loop(1, GROUP, lambda k: rows_to(k).start())
    loop(1, GROUP, lambda k: share(k).wait_recv())
    load = info_out[0]
    for h in range(1, GROUP):
        load = load + info_out[h]
    most[0] = load
    loop(1, planes, lambda k: top(k).start())
    loop(1, planes, lambda k: top(k).wait_recv())
    for k in range(1, planes):
        load = jnp.maximum(load, most[k])
    largest = jnp.max(jnp.where(lane < GROUP, load, 0))
    choice = jnp.int32(0)
    for cap in CAPACITIES[:-1]:
        choice = choice + (largest > cap).astype(i32)
    choice_ref[0] = choice
    loop(1, GROUP, lambda k: share(k).wait_send())
    loop(1, planes, lambda k: top(k).wait_send())
    local.wait()
    loop(1, GROUP, lambda k: rows_to(k).wait())


def exchange(tokens, lengths, members):
    seqs = lengths.shape[0]
    rows, width = tokens.shape
    rounds = rows // (seqs * GROUP * TILE)
    planes = members // GROUP
    slots = jax.ShapeDtypeStruct((GROUP, seqs, rounds, TILE, width), tokens.dtype)
    anywhere = pl.BlockSpec(memory_space=pl.ANY)
    smem = pl.BlockSpec(memory_space=pltpu.SMEM)
    tok, shared, choice = pl.pallas_call(
        functools.partial(exchange_kernel, planes),
        out_shape=(
            slots, jax.ShapeDtypeStruct((GROUP, 1, 128), i32), jax.ShapeDtypeStruct((1,), i32)
        ),
        in_specs=[smem, anywhere],
        out_specs=(anywhere, pl.BlockSpec(memory_space=pltpu.VMEM), smem),
        scratch_shapes=[
            pltpu.VMEM((1, 128), i32),
            pltpu.VMEM((planes, 1, 128), i32),
            pltpu.SemaphoreType.DMA((1,)),
            pltpu.SemaphoreType.DMA((GROUP,)),
            pltpu.SemaphoreType.DMA((GROUP,)),
            pltpu.SemaphoreType.DMA((GROUP,)),
            pltpu.SemaphoreType.DMA((GROUP,)),
            pltpu.SemaphoreType.DMA((planes,)),
            pltpu.SemaphoreType.DMA((planes,)),
        ],
        compiler_params=pltpu.CompilerParams(collective_id=0, has_side_effects=True),
        name="exchange",
    )(lengths, tokens.reshape(seqs, rounds, GROUP, TILE, width))
    return tok.reshape(rows, width), shared, choice[0]


def layer_kernel(
    cap, split, seqs, rounds,
    info_ref, tok_slots, gain_in, cot_ref, wg_ref, wu_ref, wd_ref,
    out_ref,
    wgu, wd, cot_slots, gain_ref, place_ref, acc, half, counts_ref, starts_ref,
    full, hidden, act, dact, both, ggug, scale_ref, mean_ref, send, recv, back,
    w_sem, in_send, in_recv, ag_send, ag_recv, rs_send, rs_recv, out_send, out_recv,
):
    dp = lax.axis_index("dp")
    tensor = lax.axis_index("tensor")
    base = dp // GROUP * GROUP
    own = dp % GROUP
    width = tok_slots.shape[1]
    parts = full.shape[2] // width
    units = wd_ref.shape[0]
    seg = rounds * TILE
    pieces = units // 128
    early, late = pl.ds(0, split), pl.ds(split, cap - split)

    def loop(low, high, step):
        def body(n, carry):
            step(n)
            return carry

        lax.fori_loop(low, high, body, 0)

    def chunk(c, size=width):
        return pl.ds(pl.multiple_of(c * size, size), size)

    def at(k):
        return chunk(tensor ^ k)

    def weight_copy(j, source, side):
        return pltpu.make_async_copy(
            source.at[:, chunk(j, 128)],
            wgu.at[:, pl.ds(pl.multiple_of(j * 256 + side * 128, 128), 128)],
            w_sem.at[2 * j + side],
        )

    down_copy = pltpu.make_async_copy(wd_ref, wd.at[pl.ds(0, units)], w_sem.at[2 * pieces])

    barrier = pltpu.get_barrier_semaphore()
    loop(1, 5, lambda k: signal(barrier, dp, tensor ^ k))
    loop(1, GROUP, lambda k: signal(barrier, base + (own + k) % GROUP, tensor))

    keep = pltpu.make_async_copy(cot_ref.at[:, :, 0], cot_slots.at[0], in_send.at[0])
    keep.start()

    def cot_in(k):
        return remote(
            cot_ref.at[:, :, k], cot_slots.at[k], in_send.at[k], in_recv.at[k],
            base + (own + k) % GROUP, tensor,
        )

    gain_ref[...] = gain_in[...].astype(f32).reshape(1, -1)
    spare = wd.shape[0] - units
    if spare:
        wd[pl.ds(units, spare), :] = jnp.zeros((spare, wd.shape[1]), bf16)
        hidden[:, pl.ds(units, spare)] = jnp.zeros((cap, spare), bf16)

    slot_rows = GROUP * seqs * seg
    lane = lax.broadcasted_iota(i32, (1, slot_rows), 1)
    place_ref[...] = jnp.full((1, slot_rows), -1, i32)

    def locate(m, total):
        k, s = m // seqs, m % seqs
        count = tile_count(info_ref[(own - k + GROUP) % GROUP, 0, GROUP + s], k)
        counts_ref[m] = count
        starts_ref[m] = total
        inside = lane - m * seg
        place_ref[...] = jnp.where(
            (inside >= 0) & (inside < count), inside + total, place_ref[...]
        )
        return total + count

    lax.fori_loop(0, GROUP * seqs, locate, jnp.int32(0))

    def accumulate(total, depth, term):
        if cap <= LARGE:
            total[...] = term(pl.ds(0, depth))
            return
        total[...] = jnp.zeros_like(total)

        def step(c):
            total[...] += term(chunk(c))

        loop(0, depth // width, step)

    def compact(i, slots):
        def term(c):
            row = lax.broadcasted_iota(i32, (cap, c.size), 0)
            picks = jnp.where(row == place_ref[:, c], 1.0, 0.0).astype(bf16)
            return jnp.dot(picks, slots[c, :], preferred_element_type=f32)

        accumulate(acc, slot_rows, term)
        full[i, :, at(0)] = acc[...].astype(bf16)

    def first_hop(i, k):
        return remote(
            full.at[i, :, at(0)], full.at[i, :, at(0)],
            ag_send.at[i, k], ag_recv.at[i, k], dp, tensor ^ k,
        )

    def to_y(i, k):
        return remote(
            full.at[i, early, at(4)], full.at[i, early, at(4)],
            ag_send.at[i, 4 + k], ag_recv.at[i, 4 + k], dp, tensor ^ k,
        )

    def to_z(i, k):
        return remote(
            full.at[i, late, at(k)], full.at[i, late, at(k)],
            ag_send.at[i, 7 + k], ag_recv.at[i, 7 + k], dp, tensor ^ 4,
        )

    def pass_from_z(i):
        first_hop(i, 4).wait_recv()
        loop(1, 4, lambda k: to_y(i, k).start())

    def pass_from_y(i):
        def step(k):
            first_hop(i, k).wait_recv()
            to_z(i, k).start()

        loop(1, 4, step)

    def arrive(i):
        def step(k):
            to_y(i, k).wait_recv()
            to_z(i, k).wait_recv()

        loop(1, 4, step)

    compact(0, tok_slots)
    pl.semaphore_wait(barrier, 4 + GROUP - 1)
    loop(0, 4, lambda n: first_hop(0, 4 - n).start())
    loop(1, GROUP, lambda k: cot_in(k).start())

    def fetch(j):
        weight_copy(j, wg_ref, 0).start()
        weight_copy(j, wu_ref, 1).start()

    loop(0, pieces, fetch)
    down_copy.start()
    pass_from_z(0)
    keep.wait()
    loop(1, GROUP, lambda k: cot_in(k).wait_recv())
    compact(1, cot_slots.reshape(slot_rows, width))
    pass_from_y(0)
    loop(0, 4, lambda n: first_hop(1, 4 - n).start())
    arrive(0)

    mean_ref[...] = jnp.zeros_like(mean_ref)

    def square(b):
        x = full[0, :, chunk(b, 128)].astype(f32)
        mean_ref[...] += x * x

    loop(0, parts * width // 128, square)
    total_sq = jnp.sum(mean_ref[...], axis=1, keepdims=True)
    scaler = lax.rsqrt(total_sq * (1.0 / (parts * width)) + EPSILON)
    scale_ref[...] = jnp.broadcast_to(scaler, (cap, 128))
    normed = ggug

    def norm(b):
        here = chunk(b, 128)
        x = full[0, :, here].astype(f32)
        normed[:, here] = (x * scale_ref[...] * gain_ref[:, here]).astype(bf16)

    loop(0, parts * width // 128, norm)

    def fetched(j):
        weight_copy(j, wg_ref, 0).wait()
        weight_copy(j, wu_ref, 1).wait()

    loop(0, pieces, fetched)
    down_copy.wait()
    pass_from_z(1)

    def forward(j):
        here = chunk(j, 128)
        accumulate(
            acc, parts * width,
            lambda c: jnp.dot(
                normed[:, c], wgu[c, chunk(j, 256)], preferred_element_type=f32
            ),
        )
        gate, up = acc[:, :128], acc[:, 128:]
        sigmoid = jax.nn.sigmoid(gate)
        silu = gate * sigmoid
        slope = up * sigmoid * (1.0 + gate * (1.0 - sigmoid))
        hidden[:, here] = (silu * up).astype(bf16)
        act[:, here] = silu
        dact[:, here] = slope
        both[:, here] = slope * gate + silu * up

        @pl.when(j == CHECK_AT)
        def _():
            pass_from_y(1)

    loop(0, pieces, forward)

    def early_copy(i, slot, peer):
        return remote(
            send.at[i, slot, early], recv.at[i, slot, early],
            rs_send.at[i, 0, slot], rs_recv.at[i, 0, slot], dp, tensor ^ peer,
        )

    def late_copy(i, slot, peer):
        return remote(
            send.at[i, slot, late], recv.at[i, slot, late],
            rs_send.at[i, 1, slot], rs_recv.at[i, 1, slot], dp, tensor ^ peer,
        )

    def scatter_first(i, part):
        def step(n):
            k = (n + 4) % parts
            part(k)

            @pl.when(k >= 4)
            def _():
                late_copy(i, k, 4).start()

            @pl.when((k > 0) & (k != 4))
            def _():
                early_copy(i, k, k % 4).start()

        loop(1, parts + 1, step)

    def scatter_second(i):
        acc[early, :] = send[i, 4, early].astype(f32)

        def across(k):
            early_copy(i, 4 + k, k).wait_recv()
            acc[early, :] += recv[i, 4 + k, early].astype(f32)

        loop(1, 4, across)
        send[i, 4, early] = acc[early, :].astype(bf16)
        early_copy(i, 4, 4).start()

        def along(k):
            late_copy(i, 4 + k, 4).wait_recv()
            pair = send[i, k, late].astype(f32) + recv[i, 4 + k, late].astype(f32)
            send[i, k, late] = pair.astype(bf16)
            late_copy(i, k, k).start()

        loop(1, 4, along)

    def layer_part(k):
        accumulate(
            acc, units if cap <= LARGE else hidden.shape[1],
            lambda c: jnp.dot(hidden[:, c], wd[c, at(k)], preferred_element_type=f32),
        )
        send[0, k] = acc[...].astype(bf16)

    scatter_first(0, layer_part)
    arrive(1)

    mean_ref[...] = jnp.zeros_like(mean_ref)

    def backward(j):
        here = chunk(j, 128)
        accumulate(
            half, parts * width,
            lambda c: lax.dot_general(
                full[1, :, c], wd[here, c], NT, preferred_element_type=f32
            ),
        )
        hgrad = half[...]
        ggug[:, pl.ds(pl.multiple_of(j * 256, 256), 128)] = (hgrad * dact[:, here]).astype(bf16)
        ggug[:, pl.ds(pl.multiple_of(j * 256 + 128, 128), 128)] = (
            hgrad * act[:, here]
        ).astype(bf16)
        mean_ref[...] += hgrad * both[:, here]

    loop(0, pieces, backward)
    mean = jnp.sum(mean_ref[...], axis=1, keepdims=True) * (1.0 / (parts * width))
    mean_ref[...] = jnp.broadcast_to(mean, (cap, 128)) * scale_ref[...]
    scatter_second(0)

    def grad_part(k):
        accumulate(
            acc, 2 * units,
            lambda c: lax.dot_general(
                ggug[:, c], wgu[at(k), c], NT, preferred_element_type=f32
            ),
        )
        unit_part = full[0, :, at(k)].astype(f32) * mean_ref[:, :1]
        send[1, k] = (scale_ref[:, :1] * (acc[...] * gain_ref[:, at(k)] - unit_part)).astype(bf16)

    scatter_first(1, grad_part)

    def stay(i):
        return pltpu.make_async_copy(back.at[i, 0], out_ref.at[i, :, :, 0], out_send.at[i, 0])

    def way_home(i, k):
        return remote(
            back.at[i, k], out_ref.at[i, :, :, k], out_send.at[i, k], out_recv.at[i, k],
            base + (own - k + GROUP) % GROUP, tensor,
        )

    def finish(i):
        @pl.when(i == 1)
        def _():
            scatter_second(1)

        acc[...] = full[i, :, at(0)].astype(f32) + send[i, 0].astype(f32)

        def add_early(k):
            early_copy(i, k, k).wait_recv()
            acc[early, :] += recv[i, k, early].astype(f32)

        loop(1, 5, add_early)

        def add_late(n):
            k = 5 - n
            late_copy(i, k, k).wait_recv()
            acc[late, :] += recv[i, k, late].astype(f32)

        loop(1, 5, add_late)
        hidden[:, :width] = acc[...].astype(bf16)

        def expand(n):
            k = (n + 3) % GROUP
            inside = lax.broadcasted_iota(i32, (seqs * seg, 1), 0)
            here = jnp.full((seqs * seg, 1), -1, i32)
            for s in range(seqs):
                pos = inside - s * seg
                m = k * seqs + s
                here = jnp.where((pos >= 0) & (pos < counts_ref[m]), pos + starts_ref[m], here)
            column = lax.broadcasted_iota(i32, (seqs * seg, cap), 1)
            spread = jnp.where(column == here, 1.0, 0.0).astype(bf16)
            rows = jnp.dot(spread, hidden[:, :width], preferred_element_type=f32)
            back[i, k] = rows.reshape(seqs, rounds, TILE, width).astype(bf16)

            @pl.when(k > 0)
            def _():
                way_home(i, k).start()

        loop(0, GROUP, expand)
        stay(i).start()

    loop(0, 2, finish)

    loop(1, GROUP, lambda k: cot_in(k).wait_send())

    def drain(i):
        loop(1, 5, lambda k: first_hop(i, k).wait_send())
        loop(1, 4, lambda k: to_y(i, k).wait_send())
        loop(1, 4, lambda k: to_z(i, k).wait_send())
        loop(1, parts, lambda k: early_copy(i, k, 1).wait_send())
        loop(1, parts, lambda k: late_copy(i, k, 1).wait_send())
        stay(i).wait()
        loop(1, GROUP, lambda k: way_home(i, k).wait())

    loop(0, 2, drain)


def layer(cap, number, info, tok, cotangent, gain, gate_weight, up_weight, down_weight, seqs):
    rows, width = tok.shape
    units, features = down_weight.shape
    padded = (units + 255) // 256 * 256
    parts = features // width
    rounds = rows // (seqs * GROUP * TILE)
    split = cap // 2 // 16 * 16
    tiled = (seqs, rounds, GROUP, TILE, width)
    slots = (GROUP, seqs, rounds, TILE, width)
    dma = pltpu.SemaphoreType.DMA
    anywhere = pl.BlockSpec(memory_space=pl.ANY)
    vmem = pl.BlockSpec(memory_space=pltpu.VMEM)
    return pl.pallas_call(
        functools.partial(layer_kernel, cap, split, seqs, rounds),
        out_shape=jax.ShapeDtypeStruct((2,) + tiled, bf16),
        in_specs=[pl.BlockSpec(memory_space=pltpu.SMEM), vmem, vmem] + [anywhere] * 4,
        out_specs=anywhere,
        scratch_shapes=[
            pltpu.VMEM((features, 2 * units), bf16),
            pltpu.VMEM((padded, features), bf16),
            pltpu.VMEM(slots, bf16),
            pltpu.VMEM((1, features), f32),
            pltpu.VMEM((1, rows), i32),
            pltpu.VMEM((cap, width), f32),
            pltpu.VMEM((cap, 128), f32),
            pltpu.SMEM((GROUP * seqs,), i32),
            pltpu.SMEM((GROUP * seqs,), i32),
            pltpu.VMEM((2, cap, features), bf16),
            pltpu.VMEM((cap, padded), bf16),
            pltpu.VMEM((cap, units), f32),
            pltpu.VMEM((cap, units), f32),
            pltpu.VMEM((cap, units), f32),
            pltpu.VMEM((cap, max(features, 2 * units)), bf16),
            pltpu.VMEM((cap, 128), f32),
            pltpu.VMEM((cap, 128), f32),
            pltpu.VMEM((2, parts, cap, width), bf16),
            pltpu.VMEM((2, parts, cap, width), bf16),
            pltpu.VMEM((2,) + slots, bf16),
            dma((2 * (units // 128) + 1,)),
            dma((GROUP,)),
            dma((GROUP,)),
            dma((2, 11)),
            dma((2, 11)),
            dma((2, 2, parts)),
            dma((2, 2, parts)),
            dma((2, GROUP)),
            dma((2, GROUP)),
        ],
        compiler_params=pltpu.CompilerParams(
            collective_id=number, has_side_effects=True, vmem_limit_bytes=62 << 20
        ),
        name=f"layer_{cap}",
    )(info, tok, gain, cotangent.reshape(tiled), gate_weight, up_weight, down_weight)


def shards(tokens, gain, gate_weight, up_weight, down_weight, cotangent, lengths):
    tok, info, choice = exchange(tokens, lengths, lax.axis_size("dp"))

    def sized(number, cap):
        return lambda: layer(
            cap, number, info, tok, cotangent, gain, gate_weight, up_weight, down_weight,
            lengths.shape[0],
        )

    out = lax.switch(choice, [sized(i + 1, cap) for i, cap in enumerate(CAPACITIES)])
    return out[0].reshape(tokens.shape), out[1].reshape(tokens.shape)


def solution(mesh):
    placed = (
        P("dp", "tensor"),
        P(),
        P(None, "tensor"),
        P(None, "tensor"),
        P("tensor", None),
        P("dp", "tensor"),
        P("dp"),
    )
    return jax.shard_map(
        shards,
        mesh=mesh,
        in_specs=placed,
        out_specs=(P("dp", "tensor"), P("dp", "tensor")),
        check_vma=False,
    )
```

time: 375 us -> 82.4 us (0.22)
  waiting for transfers between devices: 216 us -> 0 us
  Pallas kernels: 0 us -> 79.7 us
  blocking collectives: 45.5 us -> 0 us
  starting transfers between devices: 32.6 us -> 0 us
  local copies, waits for them, and re-layouts: 25.7 us -> 1.08 us
  other arithmetic: 20.8 us -> 0 us
  matrix products: 16.5 us -> 0 us
  between operations: 16.7 us -> 1.21 us
    psum x1 -> x0, waiting for transfers between devices: 82.7 us -> none  [layer_core(): normed_grad = lax.psum(normed_terms, 'tensor')]
    pallas_call x0 -> x2, Pallas kernels: none -> 79.7 us  [the longest x1 60.6 us: layer(): pl.pallas_call(functools.partial(layer_kernel, cap, split, seqs, rounds),...]
    all_gather x2 -> x0, waiting for transfers between devices: 65.5 us -> none  [the longest x1 33 us: layer_core(): lax.all_gather(cotan_part, 'tensor', axis=1, tiled=True)]
    reduce_scatter x1 -> x0, waiting for transfers between devices: 35.2 us -> none  [layer_core(): lax.psum_scatter(layer_terms.astype(jnp.bfloat16), 'tensor', scatter_dime...]
    all_to_all x3 -> x0, starting transfers between devices: 32.2 us -> none  [the longest x1 14.2 us: shards(): lax.all_to_all(unpack_slots(layer_packed), 'dp', split_axis=0, concat_axi...]
    all_to_all x3 -> x0, waiting for transfers between devices: 31.5 us -> none  [the longest x1 18.1 us: shards(): lax.all_to_all(pack_rows(tokens), 'dp', split_axis=0, concat_axis=0, tile...]
    all_to_all x1 -> x0, blocking collectives: 26.9 us -> none  [shards(): lax.all_to_all(pack_rows(cotangent), 'dp', split_axis=0, concat_axis=0, t...]
    unnamed x1 -> x0, blocking collectives: 18.6 us -> none
  transfers between devices with their start and end apart: 7 -> 0, of which waited for: 6 -> 0; matrix products, arithmetic and copies ran while one was open for 9% -> 0% of each run, Pallas kernels for 0% -> 0%
where the time goes in v3:
time: 82.4 us; the launch traced here: 82.3 us
  Pallas kernels  79.7 us (97%)
  between operations  1.21 us (1%)
  local copies, waits for them, and re-layouts  1.08 us (1%)
    pallas_call x1, Pallas kernels, layer(): pl.pallas_call(functools.partial(layer_kernel, cap, split, seqs, rounds),...  60.6 us
    pallas_call x1, Pallas kernels, exchange(): pl.pallas_call(functools.partial(exchange_kernel, planes), out_shape=(slo...  19.1 us

profile of v3, /device:TPU:1, one launch (start us, length us, event | category | flops | bytes accessed | tf_op | source)
XLA Modules:
  0.0 82.3 jit_solution(3177466735451778207)
XLA Ops:
  0.6 19.1 %exchange.1 = (bf16[8,2,8,8,256]{4,3,2,1,0:T(8,128)(2,1)S(1)}, s32[8,1,128]{2,1,0:T(1,128)S(1)}, s32[1]{0:T(128)}) custom-call(s32[2]{0:T(128)} %len_ref.1, bf16[2,8,8,8,256]{4,3,2,1,0:T(8,128)(2,1)} %bitcast.20), custom_call_target="tpu_custom_call" | custom-call | tf_op jit(solution)/shard_map/exchange/pallas_call | solution.py:121
  20.3 60.9 %conditional.1 = (bf16[2,2,8,8,8,256]{5,4,3,2,1,0:T(8,128)(2,1)S(1)}) conditional(s32[]{:T(128)} %bitcast.6, (bf16[1024,256]{1,0:T(8,128)(2,1)}, s32[8,1,128]{2,1,0:T(1,128)S(1)}, bf16[1024,256]{1,0:T(8,128)(2,1)S(1)}, bf16[2048]{0:T(1024)(128)(2,1)}, bf16[2048,896]{1,0:T(8,128)(2,1)}, ...), branch_computations={%region_0.0_spmd, %region_1.0_spmd, %region_2.0_spmd, %region_3.0_... | conditional | bytes 8 | solution.py:567
  20.4 60.6 %layer_304.1 = bf16[2,2,8,8,8,256]{5,4,3,2,1,0:T(8,128)(2,1)S(1)} custom-call(s32[8,1,128]{2,1,0:T(1,128)S(1)} %get-tuple-element.34.info_ref, bf16[1024,256]{1,0:T(8,128)(2,1)S(1)} %get-tuple-element.48.tok_slots, bf16[2048]{0:T(1024)(128)(2,1)} %get-tuple-element.70.gain_in, bf16[2,8,8,8,256]{4,3,2,1,0:T(8,128)(2,1)} %bitcast.10, ...), custom_call_target="tpu_custom_call" | custom-call | tf_op jit(solution)/shard_map/cond/branch_0_fun/layer_304/pallas_call | solution.py:515
  81.2 1.1 %fusion = (bf16[1,2,8,8,8,256]{5,4,3,2,1,0:T(8,128)(2,1)}, bf16[1,2,8,8,8,256]{5,4,3,2,1,0:T(8,128)(2,1)}) fusion(bf16[2,2,8,8,8,256]{5,4,3,2,1,0:T(8,128)(2,1)S(1)} %get-tuple-element.121), kind=kLoop, calls=%fused_computation | loop fusion | bytes 2097152 | tf_op jit(solution)/shard_map/slice | solution.py:568

commit v4 on v3

--- a/solution.py
+++ b/solution.py
@@ -143,7 +143,7 @@
 
 
 def layer_kernel(
-    cap, split, seqs, rounds,
+    cap, split, cut, seqs, rounds,
     info_ref, tok_slots, gain_in, cot_ref, wg_ref, wu_ref, wd_ref,
     out_ref,
     wgu, wd, cot_slots, gain_ref, place_ref, acc, half, counts_ref, starts_ref,
@@ -245,6 +245,13 @@
             ag_send.at[i, k], ag_recv.at[i, k], dp, tensor ^ k,
         )
 
+    def ring(i, k):
+        rows = early if k == 1 else late
+        return remote(
+            full.at[i, rows, at(k)], full.at[i, rows, at(k)],
+            ag_send.at[i, 10 + k], ag_recv.at[i, 10 + k], dp, tensor ^ (4 - k),
+        )
+
     def to_y(i, k):
         return remote(
             full.at[i, early, at(4)], full.at[i, early, at(4)],
@@ -257,18 +264,25 @@
             ag_send.at[i, 7 + k], ag_recv.at[i, 7 + k], dp, tensor ^ 4,
         )
 
-    def pass_from_z(i):
+    def set_out(i):
+        for k in (4, 1, 3):
+            first_hop(i, k).start()
+
+    def pass_on(i):
+        for k in (1, 3):
+            first_hop(i, k).wait_recv()
+            ring(i, k).start()
+            to_z(i, k).start()
         first_hop(i, 4).wait_recv()
         loop(1, 4, lambda k: to_y(i, k).start())
 
-    def pass_from_y(i):
-        def step(k):
-            first_hop(i, k).wait_recv()
-            to_z(i, k).start()
-
-        loop(1, 4, step)
+    def pass_last(i):
+        ring(i, 3).wait_recv()
+        to_z(i, 2).start()
 
     def arrive(i):
+        ring(i, 1).wait_recv()
+
         def step(k):
             to_y(i, k).wait_recv()
             to_z(i, k).wait_recv()
@@ -277,7 +291,7 @@
 
     compact(0, tok_slots)
     pl.semaphore_wait(barrier, 4 + GROUP - 1)
-    loop(0, 4, lambda n: first_hop(0, 4 - n).start())
+    set_out(0)
     loop(1, GROUP, lambda k: cot_in(k).start())
 
     def fetch(j):
@@ -286,12 +300,12 @@
 
     loop(0, pieces, fetch)
     down_copy.start()
-    pass_from_z(0)
+    pass_on(0)
     keep.wait()
     loop(1, GROUP, lambda k: cot_in(k).wait_recv())
     compact(1, cot_slots.reshape(slot_rows, width))
-    pass_from_y(0)
-    loop(0, 4, lambda n: first_hop(1, 4 - n).start())
+    pass_last(0)
+    set_out(1)
     arrive(0)
 
     mean_ref[...] = jnp.zeros_like(mean_ref)
@@ -319,7 +333,7 @@
 
     loop(0, pieces, fetched)
     down_copy.wait()
-    pass_from_z(1)
+    pass_on(1)
 
     def forward(j):
         here = chunk(j, 128)
@@ -340,19 +354,21 @@
 
         @pl.when(j == CHECK_AT)
         def _():
-            pass_from_y(1)
+            pass_last(1)
 
     loop(0, pieces, forward)
 
-    def early_copy(i, slot, peer):
-        return remote(
-            send.at[i, slot, early], recv.at[i, slot, early],
+    upper, lower = pl.ds(0, cut), pl.ds(cut, cap - cut)
+
+    def upper_copy(i, slot, peer):
+        return remote(
+            send.at[i, slot, upper], recv.at[i, slot, upper],
             rs_send.at[i, 0, slot], rs_recv.at[i, 0, slot], dp, tensor ^ peer,
         )
 
-    def late_copy(i, slot, peer):
-        return remote(
-            send.at[i, slot, late], recv.at[i, slot, late],
+    def lower_copy(i, slot, peer):
+        return remote(
+            send.at[i, slot, lower], recv.at[i, slot, lower],
             rs_send.at[i, 1, slot], rs_recv.at[i, 1, slot], dp, tensor ^ peer,
         )
 
@@ -363,30 +379,30 @@
 
             @pl.when(k >= 4)
             def _():
-                late_copy(i, k, 4).start()
+                lower_copy(i, k, 4).start()
 
             @pl.when((k > 0) & (k != 4))
             def _():
-                early_copy(i, k, k % 4).start()
+                upper_copy(i, k, k % 4).start()
 
         loop(1, parts + 1, step)
 
     def scatter_second(i):
-        acc[early, :] = send[i, 4, early].astype(f32)
+        acc[upper, :] = send[i, 4, upper].astype(f32)
 
         def across(k):
-            early_copy(i, 4 + k, k).wait_recv()
-            acc[early, :] += recv[i, 4 + k, early].astype(f32)
+            upper_copy(i, 4 + k, k).wait_recv()
+            acc[upper, :] += recv[i, 4 + k, upper].astype(f32)
 
         loop(1, 4, across)
-        send[i, 4, early] = acc[early, :].astype(bf16)
-        early_copy(i, 4, 4).start()
+        send[i, 4, upper] = acc[upper, :].astype(bf16)
+        upper_copy(i, 4, 4).start()
 
         def along(k):
-            late_copy(i, 4 + k, 4).wait_recv()
-            pair = send[i, k, late].astype(f32) + recv[i, 4 + k, late].astype(f32)
-            send[i, k, late] = pair.astype(bf16)
-            late_copy(i, k, k).start()
+            lower_copy(i, 4 + k, 4).wait_recv()
+            pair = send[i, k, lower].astype(f32) + recv[i, 4 + k, lower].astype(f32)
+            send[i, k, lower] = pair.astype(bf16)
+            lower_copy(i, k, k).start()
 
         loop(1, 4, along)
 
@@ -450,18 +466,18 @@
 
         acc[...] = full[i, :, at(0)].astype(f32) + send[i, 0].astype(f32)
 
-        def add_early(k):
-            early_copy(i, k, k).wait_recv()
-            acc[early, :] += recv[i, k, early].astype(f32)
-
-        loop(1, 5, add_early)
-
-        def add_late(n):
+        def add_upper(k):
+            upper_copy(i, k, k).wait_recv()
+            acc[upper, :] += recv[i, k, upper].astype(f32)
+
+        loop(1, 5, add_upper)
+
+        def add_lower(n):
             k = 5 - n
-            late_copy(i, k, k).wait_recv()
-            acc[late, :] += recv[i, k, late].astype(f32)
-
-        loop(1, 5, add_late)
+            lower_copy(i, k, k).wait_recv()
+            acc[lower, :] += recv[i, k, lower].astype(f32)
+
+        loop(1, 5, add_lower)
         hidden[:, :width] = acc[...].astype(bf16)
 
         def expand(n):
@@ -489,11 +505,14 @@
     loop(1, GROUP, lambda k: cot_in(k).wait_send())
 
     def drain(i):
-        loop(1, 5, lambda k: first_hop(i, k).wait_send())
+        for k in (1, 3, 4):
+            first_hop(i, k).wait_send()
+        for k in (1, 3):
+            ring(i, k).wait_send()
         loop(1, 4, lambda k: to_y(i, k).wait_send())
         loop(1, 4, lambda k: to_z(i, k).wait_send())
-        loop(1, parts, lambda k: early_copy(i, k, 1).wait_send())
-        loop(1, parts, lambda k: late_copy(i, k, 1).wait_send())
+        loop(1, parts, lambda k: upper_copy(i, k, 1).wait_send())
+        loop(1, parts, lambda k: lower_copy(i, k, 1).wait_send())
         stay(i).wait()
         loop(1, GROUP, lambda k: way_home(i, k).wait())
 
@@ -507,13 +526,14 @@
     parts = features // width
     rounds = rows // (seqs * GROUP * TILE)
     split = cap // 2 // 16 * 16
+    cut = cap * 5 // 10 // 16 * 16
     tiled = (seqs, rounds, GROUP, TILE, width)
     slots = (GROUP, seqs, rounds, TILE, width)
     dma = pltpu.SemaphoreType.DMA
     anywhere = pl.BlockSpec(memory_space=pl.ANY)
     vmem = pl.BlockSpec(memory_space=pltpu.VMEM)
     return pl.pallas_call(
-        functools.partial(layer_kernel, cap, split, seqs, rounds),
+        functools.partial(layer_kernel, cap, split, cut, seqs, rounds),
         out_shape=jax.ShapeDtypeStruct((2,) + tiled, bf16),
         in_specs=[pl.BlockSpec(memory_space=pltpu.SMEM), vmem, vmem] + [anywhere] * 4,
         out_specs=anywhere,
@@ -541,8 +561,8 @@
             dma((2 * (units // 128) + 1,)),
             dma((GROUP,)),
             dma((GROUP,)),
-            dma((2, 11)),
-            dma((2, 11)),
+            dma((2, 14)),
+            dma((2, 14)),
             dma((2, 2, parts)),
             dma((2, 2, parts)),
             dma((2, GROUP)),

time: 82.4 us -> 79.8 us (0.968)
  Pallas kernels: 79.7 us -> 77.1 us
    pallas_call x1, Pallas kernels: 60.6 us -> 57.9 us  [layer(): pl.pallas_call(functools.partial(layer_kernel, cap, split, cut, seqs, rou...]
where the time goes in v4:
time: 79.8 us; the launch traced here: 79.6 us
  Pallas kernels  77.1 us (97%)
  between operations  1.21 us (2%)
  local copies, waits for them, and re-layouts  1.08 us (1%)
    pallas_call x1, Pallas kernels, layer(): pl.pallas_call(functools.partial(layer_kernel, cap, split, cut, seqs, rou...  57.9 us
    pallas_call x1, Pallas kernels, exchange(): pl.pallas_call(functools.partial(exchange_kernel, planes), out_shape=(slo...  19.1 us

profile of v4, /device:TPU:1, one launch (start us, length us, event | category | flops | bytes accessed | tf_op | source)
XLA Modules:
  0.0 79.6 jit_solution(12602790946478849971)
XLA Ops:
  0.6 19.1 %exchange.1 = (bf16[8,2,8,8,256]{4,3,2,1,0:T(8,128)(2,1)S(1)}, s32[8,1,128]{2,1,0:T(1,128)S(1)}, s32[1]{0:T(128)}) custom-call(s32[2]{0:T(128)} %len_ref.1, bf16[2,8,8,8,256]{4,3,2,1,0:T(8,128)(2,1)} %bitcast.20), custom_call_target="tpu_custom_call" | custom-call | tf_op jit(solution)/shard_map/exchange/pallas_call | solution.py:121
  20.3 58.2 %conditional.1 = (bf16[2,2,8,8,8,256]{5,4,3,2,1,0:T(8,128)(2,1)S(1)}) conditional(s32[]{:T(128)} %bitcast.6, (bf16[1024,256]{1,0:T(8,128)(2,1)}, s32[8,1,128]{2,1,0:T(1,128)S(1)}, bf16[1024,256]{1,0:T(8,128)(2,1)S(1)}, bf16[2048]{0:T(1024)(128)(2,1)}, bf16[2048,896]{1,0:T(8,128)(2,1)}, ...), branch_computations={%region_0.0_spmd, %region_1.0_spmd, %region_2.0_spmd, %region_3.0_... | conditional | bytes 8 | solution.py:587
  20.4 57.9 %layer_336.1 = bf16[2,2,8,8,8,256]{5,4,3,2,1,0:T(8,128)(2,1)S(1)} custom-call(s32[8,1,128]{2,1,0:T(1,128)S(1)} %get-tuple-element.83.info_ref, bf16[1024,256]{1,0:T(8,128)(2,1)S(1)} %get-tuple-element.84.tok_slots, bf16[2048]{0:T(1024)(128)(2,1)} %get-tuple-element.85.gain_in, bf16[2,8,8,8,256]{4,3,2,1,0:T(8,128)(2,1)} %bitcast.11, ...), custom_call_target="tpu_custom_call" | custom-call | tf_op jit(solution)/shard_map/cond/branch_1_fun/layer_336/pallas_call | solution.py:535
  78.5 1.1 %fusion = (bf16[1,2,8,8,8,256]{5,4,3,2,1,0:T(8,128)(2,1)}, bf16[1,2,8,8,8,256]{5,4,3,2,1,0:T(8,128)(2,1)}) fusion(bf16[2,2,8,8,8,256]{5,4,3,2,1,0:T(8,128)(2,1)S(1)} %get-tuple-element.121), kind=kLoop, calls=%fused_computation | loop fusion | bytes 2097152 | tf_op jit(solution)/shard_map/slice | solution.py:588

commit v5 on v4

--- a/solution.py
+++ b/solution.py
@@ -10,7 +10,7 @@
 EPSILON = 1e-05
 GROUP = 8
 TILE = 8
-CAPACITIES = (304, 336, 368, 416, 1024)
+CAPACITIES = (320, 336, 352, 368, 400, 480, 1024)
 LARGE = 512
 CHECK_AT = 3
 MESH = pl.DeviceIdType.MESH

time: 79.8 us -> 79.9 us (level)
  no operation moved by 1% of the time
where the time goes in v5:
time: 79.9 us; the launch traced here: 79.7 us
  Pallas kernels  77.1 us (96%)
  between operations  1.27 us (2%)
  local copies, waits for them, and re-layouts  1.08 us (1%)
    pallas_call x1, Pallas kernels, layer(): pl.pallas_call(functools.partial(layer_kernel, cap, split, cut, seqs, rou...  57.9 us
    pallas_call x1, Pallas kernels, exchange(): pl.pallas_call(functools.partial(exchange_kernel, planes), out_shape=(slo...  19.1 us

profile of v5, /device:TPU:1, one launch (start us, length us, event | category | flops | bytes accessed | tf_op | source)
XLA Modules:
  0.0 79.7 jit_solution(16558585504723999642)
XLA Ops:
  0.6 19.1 %exchange.1 = (bf16[8,2,8,8,256]{4,3,2,1,0:T(8,128)(2,1)S(1)}, s32[8,1,128]{2,1,0:T(1,128)S(1)}, s32[1]{0:T(128)}) custom-call(s32[2]{0:T(128)} %len_ref.1, bf16[2,8,8,8,256]{4,3,2,1,0:T(8,128)(2,1)} %bitcast.26), custom_call_target="tpu_custom_call" | custom-call | tf_op jit(solution)/shard_map/exchange/pallas_call | solution.py:121
  20.4 58.3 %conditional.1 = (bf16[2,2,8,8,8,256]{5,4,3,2,1,0:T(8,128)(2,1)S(1)}) conditional(s32[]{:T(128)} %bitcast.8, (bf16[1024,256]{1,0:T(8,128)(2,1)}, s32[8,1,128]{2,1,0:T(1,128)S(1)}, bf16[1024,256]{1,0:T(8,128)(2,1)S(1)}, bf16[2048]{0:T(1024)(128)(2,1)}, bf16[2048,896]{1,0:T(8,128)(2,1)}, ...), branch_computations={%region_0.0_spmd, %region_1.0_spmd, %region_2.0_spmd, %region_3.0_... | conditional | bytes 8 | solution.py:587
  20.4 57.9 %layer_336.1 = bf16[2,2,8,8,8,256]{5,4,3,2,1,0:T(8,128)(2,1)S(1)} custom-call(s32[8,1,128]{2,1,0:T(1,128)S(1)} %get-tuple-element.113.info_ref, bf16[1024,256]{1,0:T(8,128)(2,1)S(1)} %get-tuple-element.114.tok_slots, bf16[2048]{0:T(1024)(128)(2,1)} %get-tuple-element.115.gain_in, bf16[2,8,8,8,256]{4,3,2,1,0:T(8,128)(2,1)} %bitcast.13, ...), custom_call_target="tpu_custom_call" | custom-call | tf_op jit(solution)/shard_map/cond/branch_1_fun/layer_336/pallas_call | solution.py:535
  78.7 1.1 %fusion = (bf16[1,2,8,8,8,256]{5,4,3,2,1,0:T(8,128)(2,1)}, bf16[1,2,8,8,8,256]{5,4,3,2,1,0:T(8,128)(2,1)}) fusion(bf16[2,2,8,8,8,256]{5,4,3,2,1,0:T(8,128)(2,1)S(1)} %get-tuple-element.165), kind=kLoop, calls=%fused_computation | loop fusion | bytes 2097152 | tf_op jit(solution)/shard_map/slice | solution.py:588
